TPU v7x, 256 devices: a whole 4x4x8 slice. The times are simulated.
256 devices in a mesh: sub: 32 (over z, y), crow: 4 (over x_hi, core), ccol: 2 (over x_lo).
Axes of the slice: x: 4 (x_hi: 2, x_lo: 2; x = x_hi * 2 + x_lo), y: 4, z: 8, core: 2. Of those that a mesh axis runs over, the one named last changes fastest.
Arguments:
- load_cases: float32 [64, 1536, 256], P('sub', 'crow', 'ccol'), may hold values from -6 to 6
- stiffness: float32 [64, 1536, 1536], P('sub', 'crow'), may hold values from -1 to 6
- local_inverse: float32 [64, 1536, 1536], P('sub', 'crow'), may hold values from -1 to 1
- coarse_basis: float32 [64, 96, 1536], P('sub', None, 'crow'), may hold values from -0.15625 to 0.15625
- coarse_inverse: float32 [6144, 6144], P(('sub', 'crow')), may hold values from -1 to 3
- coupling: float32 [64, 6, 128, 128], P('sub'), may hold values from -0.5 to 0.5
- target_local_rows: int32 [64, 6, 128], P('sub'), may hold values from 0 to 1535
- neighbour_read_rows: int32 [64, 6, 128], P('sub'), may hold values from 0 to 1535
- neighbour: int32 [64, 6], P('sub'), may hold values from 0 to 63, as said below
- counts: int32 [64], P('sub'), may hold values from 1 to 6
Outputs:
- solution: float32 [64, 1536, 256], P('sub', 'crow', 'ccol')
- residual: float32 [64, 1536, 256], P('sub', 'crow', 'ccol')
Inputs may be any that keep to these rules, and one draw needn't show every extreme that they name: neighbour[s, k] is a subdomain other than s, at most 2 away from s in the numbering. Only the first counts[s] interface blocks of subdomain s act. `target_local_rows`: rows may repeat within a block.
All inputs are finite; a program needn't handle non-finite values.
Results may differ from a plain program's by a relative error of at most 0.00013.
Values sent between devices are 32-bit elements; how exact they have to be, the bound alone decides.
A program may use at most 64 MiB of HBM per device.

v0:
```python
import jax
import jax.numpy as jnp
from jax import lax
from jax.sharding import Mesh
from jax.sharding import PartitionSpec as P

ITERS = 2
SUB = ("sub_0", "sub_1")
SUB_CROW = ("sub_0", "sub_1", "crow")


damping = 0.7
highest_mode = lax.Precision.HIGHEST


def extended(x, sides, width):
    for axis, dim in sides:
        size, length = (lax.axis_size(axis), x.shape[dim])
        up = [(i, (i + 1) % size) for i in range(size - 1)]
        down = [(j, i) for i, j in up]
        last = lax.slice_in_dim(x, length - width, length, axis=dim)
        initial = lax.slice_in_dim(x, 0, width, axis=dim)
        before = lax.ppermute(last, axis, up)
        after = lax.ppermute(initial, axis, down)
        x = jnp.concatenate([before, x, after], axis=dim)
    return x


def sent_to_all(x, axis):
    copies = jnp.broadcast_to(x, (lax.axis_size(axis), *x.shape))
    return lax.all_to_all(copies, axis, split_axis=0, concat_axis=0, tiled=True)


def laid_out(tiles, dim):
    lengths = list(tiles.shape[1:])
    lengths[dim] *= tiles.shape[0]
    return jnp.moveaxis(tiles, 0, dim).reshape(lengths)


def gathered_copies(x, axis, dim):
    tiles = sent_to_all(x, axis)
    return laid_out(tiles, dim)


def taken_together(x, axis):
    return sent_to_all(x, axis).sum(axis=0)


def whole_of(x, axes, dim):
    result = x
    for number in range(len(axes) - 1, -1, -1):
        result = lax.all_gather(result, axes[number], axis=dim, tiled=True)
    return result


def from_behind(block, axis, distance):
    devices = range(lax.axis_size(axis))
    route = [(i - distance, i) for i in devices if i - distance in devices]
    return lax.ppermute(block, axis, route)


def take_requested(full_corr, lists, sub_first):
    sub_count, local_order, case_count = full_corr.shape
    wanted = lists[:, :, -1]
    source_rows = lists[:, :, :-1]
    relative = wanted - sub_first
    present = (relative >= 0) & (relative < sub_count)
    clipped = jnp.clip(relative, 0, sub_count - 1)
    flat_rows = clipped[:, :, None] * local_order + source_rows
    picked = jnp.take(full_corr.reshape(-1, case_count), flat_rows.reshape(-1), axis=0)
    picked = picked.reshape(flat_rows.shape + (case_count,))
    return picked * present[:, :, None, None].astype(jnp.float32)


def per_device(
    load_cases,
    stiffness,
    local_inverse,
    coarse_basis,
    coarse_inverse,
    coupling,
    target_local_rows,
    neighbour_read_rows,
    neighbour,
    counts,
):
    sub_count, row_count, case_count = load_cases.shape
    local_order = stiffness.shape[2]
    mode_count = coarse_basis.shape[1]
    sub_first = lax.axis_index(SUB) * sub_count
    row_first = lax.axis_index("crow") * row_count
    target_block = jnp.arange(sub_count, dtype=jnp.int32)[:, None] * local_order
    slot_limit = jnp.max(counts)
    own_lists = jnp.concatenate([neighbour_read_rows, neighbour[:, :, None]], axis=2)
    wider_lists = extended(own_lists, ((SUB, 0),), sub_count)
    lower_lists = wider_lists[:sub_count]
    upper_lists = wider_lists[2 * sub_count :]
    solution = jnp.zeros_like(load_cases)
    residual = load_cases
    for sweep_index in range(ITERS):
        local_corr = jnp.einsum(
            "slm,smc->slc",
            local_inverse,
            gathered_copies(residual, "crow", 1),
            precision=highest_mode,
        )
        restricted = jnp.einsum("sel,slc->sec", coarse_basis, residual, precision=highest_mode)
        restricted = restricted.reshape(sub_count * mode_count, case_count)
        summed = taken_together(restricted, "crow")
        coarse_own = jnp.dot(coarse_inverse, whole_of(summed, SUB, 0), precision=highest_mode)
        coarse_mine = gathered_copies(coarse_own, "crow", 0).reshape(
            sub_count, mode_count, case_count
        )
        correction = local_corr + jnp.einsum(
            "sel,sec->slc", coarse_basis, coarse_mine, precision=highest_mode
        )
        solution = solution + damping * correction
        full_corr = gathered_copies(correction, "crow", 1)
        local_part = jnp.einsum("slm,smc->slc", stiffness, full_corr, precision=highest_mode)
        for_upper = take_requested(full_corr, upper_lists, sub_first)
        for_lower = take_requested(full_corr, lower_lists, sub_first)
        from_lower = from_behind(for_upper, SUB, 1)
        from_upper = from_behind(for_lower, SUB, -1)
        slot_sources = take_requested(full_corr, own_lists, sub_first) + from_lower + from_upper

        def fetch(slot_index):
            return slot_sources[:, slot_index]

        def add_slot(slot_index, inflow):
            sources = fetch(slot_index)
            slot_terms = jnp.einsum(
                "snm,smc->snc", coupling[:, slot_index], sources, precision=highest_mode
            )
            active_flag = (slot_index < counts).astype(jnp.float32)
            target_rows = target_block + target_local_rows[:, slot_index, :]
            return inflow.at[target_rows].add(slot_terms * active_flag[:, None, None])

        inflow = lax.fori_loop(
            0, slot_limit, add_slot, jnp.zeros((sub_count * local_order, case_count), jnp.float32)
        )
        inflow_rows = lax.dynamic_slice_in_dim(
            inflow.reshape(sub_count, local_order, case_count), row_first, row_count, 1
        )
        residual = residual - damping * (local_part - inflow_rows)
    return (solution, residual)


def solution(mesh):
    finer = Mesh(
        mesh.devices.reshape(8, 4, mesh.shape["crow"], mesh.shape["ccol"]),
        ("sub_0", "sub_1", "crow", "ccol"),
    )
    placed = (
        P(SUB, "crow", "ccol"),
        P(SUB, "crow", None),
        P(SUB, "crow", None),
        P(SUB, None, "crow"),
        P(SUB_CROW, None),
        P(SUB, None, None, None),
        P(SUB, None, None),
        P(SUB, None, None),
        P(SUB, None),
        P(SUB),
    )
    return jax.shard_map(
        per_device,
        mesh=finer,
        in_specs=placed,
        out_specs=(P(SUB, "crow", "ccol"), P(SUB, "crow", "ccol")),
        check_vma=False,
    )
```

profile of v0, /device:TPU:1, one launch (start us, length us, event | category | flops | bytes accessed | tf_op | source)
XLA Modules:
  0.0 402.8 jit_solution(6422201561983049996)
XLA Ops:
  7.2 1.6 fusion.31
  9.6 6.6 %all-to-all-start.1 = ((f32[4,192,128]{2,1,0:T(8,128)}), f32[4,192,128]{2,1,0:T(8,128)S(1)}, u32[]{:S(2)}, u32[]{:S(2)}) async-start(f32[4,192,128]{2,1,0:T(8,128)} %broadcast_in_dim.30), calls=%async_computation.1 | async-start | bytes 786432 | tf_op jit(solution)/shard_map/all_to_all | solution.py:31
  16.2 7.9 %all-to-all-done.1 = f32[4,192,128]{2,1,0:T(8,128)S(1)} async-done(((f32[4,192,128]{2,1,0:T(8,128)}), f32[4,192,128]{2,1,0:T(8,128)S(1)}, u32[]{:S(2)}, u32[]{:S(2)}) %all-to-all-start.1) | async-done | bytes 393248 | tf_op jit(solution)/shard_map/all_to_all | solution.py:31
  24.2 11.1 %all_gather.12 = f32[768,128]{1,0:T(8,128)} all-gather(f32[192,128]{1,0:T(8,128)S(1)} %reduce_sum.18), channel_id=1, replica_groups=mesh['sub_0'=8,'sub_1'=4,'crow'=4,'ccol'=2] {'sub_1'}, dimensions={0}, use_global_device_ids=true | all-gather | bytes 491520 | tf_op jit(solution)/shard_map/all_gather | solution.py:52
  36.2 2.5 collective-permute-start.2
  38.7 1.3 collective-permute-start
  41.3 8.2 %all-to-all-start = ((f32[4,2,384,128]{3,2,1,0:T(8,128)}), f32[4,2,384,128]{3,2,1,0:T(8,128)S(1)}, u32[]{:S(2)}, u32[]{:S(2)}) async-start(f32[4,2,384,128]{3,2,1,0:T(8,128)} %broadcast_in_dim.29), calls=%async_computation | async-start | bytes 3145728 | tf_op jit(solution)/shard_map/all_to_all | solution.py:31
  55.2 1.6 slice_add_fusion
  56.8 1.6 slice_add_fusion.1
  58.4 11.7 %all-to-all-done = f32[4,2,384,128]{3,2,1,0:T(8,128)S(1)} async-done(((f32[4,2,384,128]{3,2,1,0:T(8,128)}), f32[4,2,384,128]{3,2,1,0:T(8,128)S(1)}, u32[]{:S(2)}, u32[]{:S(2)}) %all-to-all-start) | async-done | bytes 1572896 | tf_op jit(solution)/shard_map/all_to_all | solution.py:31
  71.4 10.5 %all-gather.3.cloned.1.call-done = f32[6144,128]{1,0:T(8,128)} async-done(((f32[768,128]{1,0:T(8,128)}), f32[6144,128]{1,0:T(8,128)}) %all-gather.3.cloned.1.call-update) | async-done | bytes 3145744 | tf_op jit(solution)/shard_map/all_gather | solution.py:52
  81.9 3.9 convolution_bitcast_fusion.4
  86.4 6.0 %all-to-all-start.2 = ((f32[4,48,128]{2,1,0:T(8,128)}), f32[4,48,128]{2,1,0:T(8,128)S(1)}, u32[]{:S(2)}, u32[]{:S(2)}) async-start(f32[4,48,128]{2,1,0:T(8,128)} %broadcast_in_dim.31), calls=%async_computation.2 | async-start | bytes 196608 | tf_op jit(solution)/shard_map/all_to_all | solution.py:31
  92.4 5.8 %fusion.30 = f32[2,384,128]{2,1,0:T(8,128)S(1)} fusion(f32[2,384,1536]{2,1,0:T(8,128)} %param.18, f32[2,1536,128]{2,1,0:T(8,128)S(1)} %bitcast.152), kind=kOutput, calls=%fused_computation.86 | convolution fusion | flops 1811939328 | bytes 6684672 | tf_op jit(solution)/shard_map/slm,smc->slc/dot_general | solution.py:101
  99.2 1.3 broadcast_in_dim.32
  100.5 4.9 %all-to-all-start.3 = ((f32[4,2,384,128]{2,3,1,0:T(8,128)}), f32[4,2,384,128]{2,3,1,0:T(8,128)S(1)}, u32[]{:S(2)}, u32[]{:S(2)}) async-start(f32[4,2,384,128]{2,3,1,0:T(8,128)} %broadcast_in_dim.32), calls=%async_computation.3 | async-start | bytes 3145728 | tf_op jit(solution)/shard_map/all_to_all | solution.py:31
  106.6 19.4 %all-to-all-done.3 = f32[4,2,384,128]{2,3,1,0:T(8,128)S(1)} async-done(((f32[4,2,384,128]{2,3,1,0:T(8,128)}), f32[4,2,384,128]{2,3,1,0:T(8,128)S(1)}, u32[]{:S(2)}, u32[]{:S(2)}) %all-to-all-start.3) | async-done | bytes 1572896 | tf_op jit(solution)/shard_map/all_to_all | solution.py:31
  127.2 1.9 copy.215
  129.0 3.7 gather_fusion.2
  132.8 3.7 gather_fusion.1
  136.4 1.5 broadcast_select_fusion.4
  138.9 4.1 %collective-permute-start.1 = (f32[2,6,128,128]{3,2,0,1:T(8,128)}, f32[2,6,128,128]{3,2,0,1:T(8,128)}, u32[]{:S(2)}, u32[]{:S(2)}) collective-permute-start(f32[2,6,128,128]{3,2,0,1:T(8,128)} %copy_multiply_fusion.4), channel_id=1, source_target_pairs={{0,8},{8,16},{16,24},{24,32},{32,40},{40,48},{48,56},{56,64},{64,7... | collective-permute-start | bytes 2359304 | tf_op jit(solution)/shard_map/ppermute | solution.py:59
  144.3 1.3 collective-permute-start.3
  145.7 3.7 gather_fusion
  149.4 2.9 copy.243
  152.5 5.9 %collective-permute-done.1 = f32[2,6,128,128]{3,2,0,1:T(8,128)} collective-permute-done((f32[2,6,128,128]{3,2,0,1:T(8,128)}, f32[2,6,128,128]{3,2,0,1:T(8,128)}, u32[]{:S(2)}, u32[]{:S(2)}) %collective-permute-start.1) | collective-permute-done | bytes 786464 | tf_op jit(solution)/shard_map/ppermute | solution.py:59
  158.4 6.0 %collective-permute-done.3 = f32[2,6,128,128]{3,2,0,1:T(8,128)} collective-permute-done((f32[2,6,128,128]{3,2,0,1:T(8,128)}, f32[2,6,128,128]{3,2,0,1:T(8,128)}, u32[]{:S(2)}, u32[]{:S(2)}) %collective-permute-start.3) | collective-permute-done | bytes 786464 | tf_op jit(solution)/shard_map/ppermute | solution.py:59
  164.4 2.4 fusion.27
  167.5 31.4 %while.22 = (s32[]{:T(128)}, f32[3072,128]{1,0:T(8,128)S(1)}, s32[]{:T(128)}, s32[2,6,128]{2,0,1:T(2,128)}, f32[2,6,128,128]{3,2,0,1:T(8,128)}, /*index=5*/f32[2...) while((s32[]{:T(128)}, f32[3072,128]{1,0:T(8,128)S(1)}, s32[]{:T(128)}, ...), condition=%wide.region_4.6_spmd.clone, body=%wide.region_2.0_spmd.clone.sunk | while | flops 50398216 | bytes 790719 | solution.py:138
  170.1 2.5 scatter_fusion
  175.2 2.5 scatter_fusion
  180.3 2.5 scatter_fusion
  185.4 2.5 scatter_fusion
  190.5 2.5 scatter_fusion
  195.6 2.5 scatter_fusion
  198.9 6.9 %fusion.20 = f32[2,384,128]{2,1,0:T(8,128)S(1)} fusion(f32[2,384,128]{2,1,0:T(8,128)} %param.16, f32[2,1536,128]{1,2,0:T(8,128)} %bitcast.155, f32[2,384,1536]{2,1,0:T(8,128)} %param.17, f32[2,1536,128]{2,1,0:T(8,128)S(1)} %bitcast.143, s32[]{:T(128)S(6)} %select_n.41), kind=kOutput, calls=%fused_computation.40 | convolution fusion | flops 1812234240 | bytes 7471108 | tf_op jit(solution)/shard_map/slm,smc->slc/dot_general | solution.py:119
  206.3 12.4 %all_to_all.42 = f32[4,192,128]{2,1,0:T(8,128)S(1)} all-to-all(f32[4,192,128]{2,1,0:T(8,128)S(1)} %broadcast_in_dim.59), channel_id=1, replica_groups=mesh['sub_0'=8,'sub_1'=4,'crow'=4,'ccol'=2] {'crow'}, dimensions={0} | all-to-all | bytes 786432 | tf_op jit(solution)/shard_map/all_to_all | solution.py:31
  218.7 12.4 %all_gather.14 = f32[768,128]{1,0:T(8,128)} all-gather(f32[192,128]{1,0:T(8,128)S(1)} %reduce_sum.19), channel_id=1, replica_groups=mesh['sub_0'=8,'sub_1'=4,'crow'=4,'ccol'=2] {'sub_1'}, dimensions={0}, use_global_device_ids=true | all-gather | bytes 491520 | tf_op jit(solution)/shard_map/all_gather | solution.py:52
  231.3 25.6 %all_to_all.40 = f32[4,2,384,128]{2,3,1,0:T(8,128)S(1)} all-to-all(f32[4,2,384,128]{2,3,1,0:T(8,128)S(1)} %broadcast_in_dim.58), channel_id=1, replica_groups=mesh['sub_0'=8,'sub_1'=4,'crow'=4,'ccol'=2] {'crow'}, dimensions={0} | all-to-all | bytes 3145728 | tf_op jit(solution)/shard_map/all_to_all | solution.py:31
  257.2 16.9 %all-gather.5.cloned.1.call-done = f32[6144,128]{1,0:T(8,128)} async-done(((f32[768,128]{1,0:T(8,128)}), f32[6144,128]{1,0:T(8,128)}) %all-gather.5.cloned.1.call-update) | async-done | bytes 3145744 | tf_op jit(solution)/shard_map/all_gather | solution.py:52
  274.1 3.9 convolution_bitcast_fusion.3
  278.6 5.5 %all-to-all-start.6 = ((f32[4,48,128]{2,1,0:T(8,128)}), f32[4,48,128]{2,1,0:T(8,128)S(1)}, u32[]{:S(2)}, u32[]{:S(2)}) async-start(f32[4,48,128]{2,1,0:T(8,128)} %broadcast_in_dim.60), calls=%async_computation.6 | async-start | bytes 196608 | tf_op jit(solution)/shard_map/all_to_all | solution.py:31
  284.1 5.8 %fusion.32 = f32[2,128,384]{1,2,0:T(8,128)S(1)} fusion(f32[2,1536,128]{1,2,0:T(8,128)S(1)} %bitcast.153, f32[2,384,1536]{2,1,0:T(8,128)} %param.18), kind=kOutput, calls=%fused_computation.88 | convolution fusion | flops 1811939328 | bytes 6684672 | tf_op jit(solution)/shard_map/slm,smc->slc/dot_general | solution.py:101
  289.9 1.6 add_multiply_fusion
  291.7 25.2 %all_to_all.41 = f32[4,2,384,128]{2,3,1,0:T(8,128)} all-to-all(f32[4,2,384,128]{2,3,1,0:T(8,128)S(1)} %broadcast_in_dim.61), channel_id=1, replica_groups=mesh['sub_0'=8,'sub_1'=4,'crow'=4,'ccol'=2] {'crow'}, dimensions={0} | all-to-all | bytes 3145728 | tf_op jit(solution)/shard_map/all_to_all | solution.py:31
  316.9 1.9 copy.233
  318.8 3.7 gather_fusion.5
  322.5 3.7 gather_fusion.4
  326.2 1.5 broadcast_select_fusion
  330.0 4.0 collective-permute-start.4
  334.0 1.3 collective-permute-start.5
  335.3 3.7 gather_fusion.3
  339.0 2.8 copy.245
  342.1 7.2 %collective-permute-done.4 = f32[2,6,128,128]{3,2,0,1:T(8,128)} collective-permute-done((f32[2,6,128,128]{3,2,0,1:T(8,128)}, f32[2,6,128,128]{3,2,0,1:T(8,128)}, u32[]{:S(2)}, u32[]{:S(2)}) %collective-permute-start.4) | collective-permute-done | bytes 786464 | tf_op jit(solution)/shard_map/ppermute | solution.py:59
  349.3 4.7 %collective-permute-done.5 = f32[2,6,128,128]{3,2,0,1:T(8,128)} collective-permute-done((f32[2,6,128,128]{3,2,0,1:T(8,128)}, f32[2,6,128,128]{3,2,0,1:T(8,128)}, u32[]{:S(2)}, u32[]{:S(2)}) %collective-permute-start.5) | collective-permute-done | bytes 786464 | tf_op jit(solution)/shard_map/ppermute | solution.py:59
  354.0 2.4 fusion.25
  357.1 31.2 %while.23 = (s32[]{:T(128)}, f32[3072,128]{1,0:T(8,128)S(1)}, s32[]{:T(128)}, s32[2,6,128]{2,0,1:T(2,128)}, f32[2,6,128,128]{3,2,0,1:T(8,128)}, /*index=5*/f32[2...) while((s32[]{:T(128)}, f32[3072,128]{1,0:T(8,128)S(1)}, s32[]{:T(128)}, ...), condition=%wide.region_8.10_spmd.clone, body=%wide.region_6.9_spmd.clone.sunk | while | flops 50398216 | bytes 790719 | solution.py:138
  359.6 2.5 scatter_fusion.1
  364.8 2.5 scatter_fusion.1
  369.9 2.5 scatter_fusion.1
  375.0 2.5 scatter_fusion.1
  380.1 2.5 scatter_fusion.1
  385.2 2.5 scatter_fusion.1
  388.3 7.6 %fusion.23 = f32[2,384,128]{2,1,0:T(8,128)} fusion(f32[2,384,128]{2,1,0:T(8,128)S(1)} %fusion.20, f32[2,1536,128]{1,2,0:T(8,128)} %bitcast.154, f32[2,384,1536]{2,1,0:T(8,128)} %param.17, f32[2,1536,128]{2,1,0:T(8,128)S(1)} %bitcast.142, s32[]{:T(128)S(6)} %select_n.41), kind=kOutput, calls=%fused_computation.43 | convolution fusion | flops 1812234240 | bytes 7471108 | tf_op jit(solution)/shard_map/slm,smc->slc/dot_general | solution.py:119
  (184 shorter events, 46.2 us)
Async XLA Ops:
  7.2 74.7 %copy-start = (f32[48,6144]{1,0:T(8,128)S(1)}, f32[48,6144]{1,0:T(8,128)}, u32[]{:S(2)}) copy-start(f32[48,6144]{1,0:T(8,128)} %param.20) | copy-start | bytes 3538948
  7.2 28.1 %copy-start.25 = (s32[2,6,128]{2,0,1:T(2,128)S(1)}, s32[2,6,128]{2,0,1:T(2,128)}, u32[]{:S(2)}) copy-start(s32[2,6,128]{2,0,1:T(2,128)} %param.23) | copy-start | bytes 18436
  8.8 26.7 %copy-start.32 = (s32[2,6]{1,0:T(2,128)S(1)}, s32[2,6]{1,0:T(2,128)}, u32[]{:S(2)}) copy-start(s32[2,6]{1,0:T(2,128)} %param.24) | copy-start | bytes 148
  8.8 31.2 %copy-start.7 = (f32[2,384,128]{2,1,0:T(8,128)S(1)}, f32[2,384,128]{2,1,0:T(8,128)}, u32[]{:S(2)}) copy-start(f32[2,384,128]{2,1,0:T(8,128)} %param.16) | copy-start | bytes 1179652
  9.6 14.6 %all-to-all-start.1 = ((f32[4,192,128]{2,1,0:T(8,128)}), f32[4,192,128]{2,1,0:T(8,128)S(1)}, u32[]{:S(2)}, u32[]{:S(2)}) async-start(f32[4,192,128]{2,1,0:T(8,128)} %broadcast_in_dim.30), calls=%async_computation.1 | async-start | bytes 786432 | tf_op jit(solution)/shard_map/all_to_all | solution.py:31
  16.2 65.6 %all-gather.3.cloned.1.call-start = ((), (), s32[]{:S(2)}) async-start(), calls=%async_computation.8 | async-start | bytes 3538944 | tf_op jit(solution)/shard_map/all_gather | solution.py:52
  36.2 17.1 %collective-permute-start.2 = (s32[2,6,129]{1,0,2:T(2,128)}, s32[2,6,129]{1,0,2:T(2,128)}, u32[]{:S(2)}, u32[]{:S(2)}) collective-permute-start(s32[2,6,129]{1,0,2:T(2,128)} %pad_add_fusion), channel_id=1, source_target_pairs={{0,8},{8,16},{16,24},{24,32},{32,40},{40,48},{48,56},{56,64},{64,7... | collective-permute-start | bytes 18584 | tf_op jit(solution)/shard_map/ppermute | solution.py:23
  38.7 15.8 %collective-permute-start = (s32[2,6,129]{1,0,2:T(2,128)}, s32[2,6,129]{1,0,2:T(2,128)}, u32[]{:S(2)}, u32[]{:S(2)}) collective-permute-start(s32[2,6,129]{1,0,2:T(2,128)} %pad_add_fusion), channel_id=1, source_target_pairs={{8,0},{16,8},{24,16},{32,24},{40,32},{48,40},{56,48},{64,56},{72,6... | collective-permute-start | bytes 18584 | tf_op jit(solution)/shard_map/ppermute | solution.py:24
  41.3 10.4 %copy-start.12 = (f32[2,6,128,128]{3,2,1,0:T(8,128)S(1)}, f32[2,6,128,128]{3,2,1,0:T(8,128)}, u32[]{:S(2)}) copy-start(f32[2,6,128,128]{3,2,1,0:T(8,128)} %param.21) | copy-start | bytes 2359300
  41.3 28.8 %all-to-all-start = ((f32[4,2,384,128]{3,2,1,0:T(8,128)}), f32[4,2,384,128]{3,2,1,0:T(8,128)S(1)}, u32[]{:S(2)}, u32[]{:S(2)}) async-start(f32[4,2,384,128]{3,2,1,0:T(8,128)} %broadcast_in_dim.29), calls=%async_computation | async-start | bytes 3145728 | tf_op jit(solution)/shard_map/all_to_all | solution.py:31
  49.7 2.9 copy-start.33
  71.4 21.0 %copy-start.3 = (f32[2,4,384,128]{3,2,1,0:T(8,128)S(1)}, f32[2,4,384,128]{3,2,1,0:T(8,128)}, u32[]{:S(2)}) copy-start(f32[2,4,384,128]{3,2,1,0:T(8,128)} %copy.208) | copy-start | bytes 4718596
  86.4 11.8 %all-to-all-start.2 = ((f32[4,48,128]{2,1,0:T(8,128)}), f32[4,48,128]{2,1,0:T(8,128)S(1)}, u32[]{:S(2)}, u32[]{:S(2)}) async-start(f32[4,48,128]{2,1,0:T(8,128)} %broadcast_in_dim.31), calls=%async_computation.2 | async-start | bytes 196608 | tf_op jit(solution)/shard_map/all_to_all | solution.py:31
  92.4 5.8 %copy-start.4 = (f32[2,96,384]{2,1,0:T(8,128)S(1)}, f32[2,96,384]{2,1,0:T(8,128)}, u32[]{:S(2)}) copy-start(f32[2,96,384]{2,1,0:T(8,128)} %param.19) | copy-start | bytes 884740
  99.0 1.5 copy-start.5
  100.5 5.6 %copy-start.14 = (s32[2,6,128]{1,0,2:T(2,128)S(1)}, s32[2,6,128]{1,0,2:T(2,128)}, u32[]{:S(2)}) copy-start(s32[2,6,128]{1,0,2:T(2,128)} %slice_add_fusion) | copy-start | bytes 18436
  100.5 5.8 %copy-start.13 = (s32[2,6,128]{1,0,2:T(2,128)S(1)}, s32[2,6,128]{1,0,2:T(2,128)}, u32[]{:S(2)}) copy-start(s32[2,6,128]{1,0,2:T(2,128)} %slice_add_fusion.1) | copy-start | bytes 18436
  100.5 25.5 %all-to-all-start.3 = ((f32[4,2,384,128]{2,3,1,0:T(8,128)}), f32[4,2,384,128]{2,3,1,0:T(8,128)S(1)}, u32[]{:S(2)}, u32[]{:S(2)}) async-start(f32[4,2,384,128]{2,3,1,0:T(8,128)} %broadcast_in_dim.32), calls=%async_computation.3 | async-start | bytes 3145728 | tf_op jit(solution)/shard_map/all_to_all | solution.py:31
  105.4 168.6 %all-gather.5.cloned.1.call-start = ((), (), s32[]{:S(2)}) async-start(), calls=%async_computation.9 | async-start | bytes 3538944 | tf_op jit(solution)/shard_map/all_gather | solution.py:52
  106.3 37.1 %copy-start.20 = (f32[2,6]{0,1:T(8,128)}, f32[2,6]{0,1:T(8,128)S(1)}, u32[]{:S(2)}) copy-start(f32[2,6]{0,1:T(8,128)S(1)} %copy.223) | copy-start | bytes 148
  106.5 31.5 %copy-start.22 = (f32[2,6]{0,1:T(8,128)}, f32[2,6]{0,1:T(8,128)S(1)}, u32[]{:S(2)}) copy-start(f32[2,6]{0,1:T(8,128)S(1)} %copy.220) | copy-start | bytes 148
  106.5 26.2 %copy-start.15 = (s32[2048]{0:T(1024)}, s32[2048]{0:T(1024)S(1)}, u32[]{:S(2)}) copy-start(s32[2048]{0:T(1024)S(1)} %pad_clamp_fusion.1) | copy-start | bytes 24580
  106.5 36.5 %copy-start.28 = (pred[1536]{0:T(1024)(128)(4,1)}, pred[1536]{0:T(1024)(128)(4,1)S(1)}, u32[]{:S(2)}) copy-start(pred[1536]{0:T(1024)(128)(4,1)S(1)} %compare_and_fusion) | copy-start | bytes 4612
  106.6 29.9 %copy-start.26 = (pred[1536]{0:T(1024)(128)(4,1)}, pred[1536]{0:T(1024)(128)(4,1)S(1)}, u32[]{:S(2)}) copy-start(pred[1536]{0:T(1024)(128)(4,1)S(1)} %compare_and_fusion.1) | copy-start | bytes 4612
  126.0 1.2 copy-start.2
  136.4 6.6 %copy-start.8 = (f32[1536,128]{1,0:T(8,128)S(1)}, f32[1536,128]{1,0:T(8,128)}, u32[]{:S(2)}) copy-start(f32[1536,128]{1,0:T(8,128)} %gather_fusion.2) | copy-start | bytes 2359300
  138.9 6.7 %copy-start.24 = (s32[1536]{0:T(1024)S(1)}, s32[1536]{0:T(1024)}, u32[]{:S(2)}) copy-start(s32[1536]{0:T(1024)} %compare_select_fusion.4) | copy-start | bytes 18436
  138.9 19.5 %collective-permute-start.1 = (f32[2,6,128,128]{3,2,0,1:T(8,128)}, f32[2,6,128,128]{3,2,0,1:T(8,128)}, u32[]{:S(2)}, u32[]{:S(2)}) collective-permute-start(f32[2,6,128,128]{3,2,0,1:T(8,128)} %copy_multiply_fusion.4), channel_id=1, source_target_pairs={{0,8},{8,16},{16,24},{24,32},{32,40},{40,48},{48,56},{56,64},{64,7... | collective-permute-start | bytes 2359304 | tf_op jit(solution)/shard_map/ppermute | solution.py:59
  144.3 20.0 %collective-permute-start.3 = (f32[2,6,128,128]{3,2,0,1:T(8,128)}, f32[2,6,128,128]{3,2,0,1:T(8,128)}, u32[]{:S(2)}, u32[]{:S(2)}) collective-permute-start(f32[2,6,128,128]{3,2,0,1:T(8,128)} %copy_multiply_fusion.3), channel_id=1, source_target_pairs={{8,0},{16,8},{24,16},{32,24},{40,32},{48,40},{56,48},{64,56},{72,6... | collective-permute-start | bytes 2359304 | tf_op jit(solution)/shard_map/ppermute | solution.py:59
  145.6 3.7 copy-start.17
  145.7 6.6 %copy-start.30 = (pred[1536]{0:T(1024)(128)(4,1)}, pred[1536]{0:T(1024)(128)(4,1)S(1)}, u32[]{:S(2)}) copy-start(pred[1536]{0:T(1024)(128)(4,1)S(1)} %compare_and_fusion.2) | copy-start | bytes 4612
  149.4 2.9 copy-start.11
  152.2 12.1 %copy-start.19 = (f32[2,6]{0,1:T(8,128)S(1)}, f32[2,6]{0,1:T(8,128)}, u32[]{:S(2)}) copy-start(f32[2,6]{0,1:T(8,128)} %copy.216) | copy-start | bytes 148
  166.8 0.7 copy-start.34
  278.6 11.3 %all-to-all-start.6 = ((f32[4,48,128]{2,1,0:T(8,128)}), f32[4,48,128]{2,1,0:T(8,128)S(1)}, u32[]{:S(2)}, u32[]{:S(2)}) async-start(f32[4,48,128]{2,1,0:T(8,128)} %broadcast_in_dim.60), calls=%async_computation.6 | async-start | bytes 196608 | tf_op jit(solution)/shard_map/all_to_all | solution.py:31
  284.1 5.8 %copy-start.6 = (f32[2,384,128]{2,1,0:T(8,128)S(1)}, f32[2,384,128]{2,1,0:T(8,128)}, u32[]{:S(2)}) copy-start(f32[2,384,128]{2,1,0:T(8,128)} %copy-done.5) | copy-start | bytes 1179652
  318.8 3.7 copy-start.16
  322.5 3.7 copy-start.29
  326.2 1.5 copy-start.21
  326.2 2.5 copy-start.9
  326.2 2.5 copy-start.27
  327.7 1.3 copy-start.23
  328.7 6.6 %copy-start.18 = (s32[2048]{0:T(1024)S(1)}, s32[2048]{0:T(1024)}, u32[]{:S(2)}) copy-start(s32[2048]{0:T(1024)} %copy-done.17) | copy-start | bytes 24580
  330.0 19.3 %collective-permute-start.4 = (f32[2,6,128,128]{3,2,0,1:T(8,128)}, f32[2,6,128,128]{3,2,0,1:T(8,128)}, u32[]{:S(2)}, u32[]{:S(2)}) collective-permute-start(f32[2,6,128,128]{3,2,0,1:T(8,128)} %copy_multiply_fusion.1), channel_id=1, source_target_pairs={{0,8},{8,16},{16,24},{24,32},{32,40},{40,48},{48,56},{56,64},{64,7... | collective-permute-start | bytes 2359304 | tf_op jit(solution)/shard_map/ppermute | solution.py:59
  334.0 20.0 %collective-permute-start.5 = (f32[2,6,128,128]{3,2,0,1:T(8,128)}, f32[2,6,128,128]{3,2,0,1:T(8,128)}, u32[]{:S(2)}, u32[]{:S(2)}) collective-permute-start(f32[2,6,128,128]{3,2,0,1:T(8,128)} %copy_multiply_fusion), channel_id=1, source_target_pairs={{8,0},{16,8},{24,16},{32,24},{40,32},{48,40},{56,48},{64,56},{72,6... | collective-permute-start | bytes 2359304 | tf_op jit(solution)/shard_map/ppermute | solution.py:59
  339.0 2.9 copy-start.10
  339.0 2.9 copy-start.31
  356.4 0.7 copy-start.35
  388.3 7.7 %copy-start.1 = (f32[48,6144]{1,0:T(8,128)S(1)}, f32[48,6144]{1,0:T(8,128)}, u32[]{:S(2)}) copy-start(f32[48,6144]{1,0:T(8,128)} %param.20) | copy-start | bytes 3538948
Sparse Core Ops, SparseCore 0:
  35.4 46.4 all-gather.2
  231.2 42.8 all-gather.4
where the time goes:
time: 406 us; the launch traced here: 403 us
  waiting for transfers between devices  90.2 us (22%)
  blocking collectives  86.7 us (21%)
  other arithmetic  60.8 us (15%)
  matrix products  53 us (13%)
  starting transfers between devices  45.7 us (11%)
  local copies, waits for them, and re-layouts  43.3 us (11%)
  between operations  14.6 us (4%)
  loops' own time  8.53 us (2%)
    all_to_all x3, blocking collectives, sent_to_all(): return lax.all_to_all(copies, axis, split_axis=0, concat_axis=0, tiled=True)  63.2 us
    all_to_all x5, waiting for transfers between devices, sent_to_all(): return lax.all_to_all(copies, axis, split_axis=0, concat_axis=0, tiled=True)  39 us
    all_to_all x5, starting transfers between devices, sent_to_all(): return lax.all_to_all(copies, axis, split_axis=0, concat_axis=0, tiled=True)  31.2 us
    scatter-add x12, other arithmetic, add_slot(): return inflow.at[target_rows].add(slot_terms * active_flag[:, None, None])  30.2 us
    all_gather x2, waiting for transfers between devices, whole_of(): result = lax.all_gather(result, axes[number], axis=dim, tiled=True)  27.4 us
    ppermute x4, waiting for transfers between devices, from_behind(): return lax.ppermute(block, axis, route)  23.7 us
    all_gather x2, blocking collectives, whole_of(): result = lax.all_gather(result, axes[number], axis=dim, tiled=True)  23.4 us
    gather x6, local copies, waits for them, and re-layouts, take_requested(): jnp.take(full_corr.reshape(-1, case_count), flat_rows.reshape(-1), axis=0)  22.1 us
  transfers between devices with their start and end apart: 13, of which 9 were waited for; matrix products, arithmetic and copies ran while one was open for 10% of the time, Pallas kernels for 0%

commit v1 on v0

v1 whole, which is shorter than its diff:
```python
import jax
import jax.numpy as jnp
from jax import lax
from jax.experimental import pallas as pl
from jax.experimental.pallas import tpu as pltpu
from jax.sharding import Mesh
from jax.sharding import PartitionSpec as P

ITERS = 2
SUB = ("sub_0", "sub_1")
SUB_CROW = ("sub_0", "sub_1", "crow")
AXES = ("sub_0", "sub_1", "crow", "ccol")

damping = 0.7
f32 = jnp.float32
bf16 = jnp.bfloat16


def split(x):
    hi = x.astype(bf16)
    lo = (x - hi.astype(f32)).astype(bf16)
    return hi, lo


def wide(x):
    hi, lo = split(x)
    return jnp.concatenate([hi, lo], axis=1)


def mm(a, b):
    return jnp.dot(a, b, preferred_element_type=f32)


def quad(acc, rows):
    return acc[:rows, :128] + acc[:rows, 128:] + acc[rows:, :128]


def halves(acc):
    return acc[:, :128] + acc[:, 128:]


def kernel(
    r_hbm, s_hbm, l_hbm, b_hbm, k_hbm, c_hbm, lists, targets,
    sol, res,
    rb, lb, bf, bt, bo, am, stage, kst, km, rhs, xs, r1, part, pin, psend, precv,
    pickm, tt, ps, fr, tm, cst, cm, rl, co48, vsum,
    ldsem, ss, rs,
):
    z, y, cr, cc = [lax.axis_index(a) for a in AXES]
    co = lax.rem(cr, 2)
    oc = lax.rem(cr + 2, 4)
    sc = cr + 1 - 2 * co
    osc = lax.rem(sc + 2, 4)
    d = z * 4 + y
    d_up = lax.rem(d + 1, 32)
    d_dn = lax.rem(d + 31, 32)
    sib = (z, y, sc, cc)
    opp = (z, y, oc, cc)
    ops = (z, y, osc, cc)
    twin = (z, y, cr, 1 - cc)
    otwin = (z, y, oc, 1 - cc)
    up = (lax.div(d_up, 4), lax.rem(d_up, 4), cr, cc)
    dn = (lax.div(d_dn, 4), lax.rem(d_dn, 4), cr, cc)

    def yat(k):
        return (z, lax.rem(y + k, 4), cr, cc)

    def zat(k):
        return (lax.rem(z + k, 8), y, cr, cc)

    counter = [0]
    pending = []

    def remote(src, dst, dev, keep=True):
        i = counter[0]
        counter[0] += 1
        c = pltpu.make_async_remote_copy(
            src_ref=src, dst_ref=dst, send_sem=ss.at[i], recv_sem=rs.at[i],
            device_id=dev, device_id_type=pl.DeviceIdType.MESH,
        )
        if keep:
            pending.append(c)
        return c

    def load(i, src, dst):
        c = pltpu.make_async_copy(src, dst, ldsem.at[i])
        c.start()
        return c

    ld_b = load(0, b_hbm, bf.at[:, cr, pl.ds(0, 96)])
    ld_r = load(1, r_hbm, rb.at[0, :, cr])
    ld_l = [load(2 + s, l_hbm.at[s], stage.at[s]) for s in range(2)]
    ld_k = load(4, k_hbm, kst)
    ld_c = load(5, c_hbm.at[co], cst)

    bar = pltpu.get_barrier_semaphore()

    def greet(devs):
        for dev in devs:
            pl.semaphore_signal(bar, inc=1, device_id=dev, device_id_type=pl.DeviceIdType.MESH)

    greet([sib, opp, ops, twin, otwin, up, dn])

    @pl.when(co == 0)
    def _():
        greet([yat(1), yat(2), yat(3), zat(1), zat(7)])
        pl.semaphore_wait(bar, 12)

    @pl.when(co == 1)
    def _():
        greet([zat(k) for k in range(1, 8)] + [yat(1), yat(3)])
        pl.semaphore_wait(bar, 16)

    def conv_matrix(m, s):
        def body(i, carry):
            rows = pl.ds(pl.multiple_of(i * 32, 32), 32)
            rows2 = pl.ds(pl.multiple_of(384 + i * 32, 32), 32)
            hi, lo = split(stage[s, rows, :])
            am[m, s, rows, :] = hi
            am[m, s, rows2, :] = lo
            return carry
        lax.fori_loop(0, 12, body, 0)

    lane = lax.broadcasted_iota(jnp.int32, (128, 128), 1)
    sub_iota = lax.broadcasted_iota(jnp.int32, (128, 128), 0)

    def build_pick(m, row_of):
        def body(k, carry):
            row = jnp.broadcast_to(row_of(k), (128, 128))
            col = jnp.transpose(row)
            rows = pl.ds(pl.multiple_of(k * 128, 128), 128)
            for t in range(12):
                pickm[m, rows, 128 * t:128 * (t + 1)] = jnp.where(
                    col == lane + 128 * t, 1.0, 0.0
                ).astype(bf16)
            return carry
        lax.fori_loop(0, 6, body, 0)

    def build_scatter(s):
        for k in range(6):
            row = jnp.broadcast_to(targets[s, k:k + 1, :], (128, 128))

            def body(t, carry):
                rows = pl.ds(pl.multiple_of(t * 128, 128), 128)
                tt[s, rows, 128 * k:128 * (k + 1)] = jnp.where(
                    row == sub_iota + 128 * t, 1.0, 0.0
                ).astype(bf16)
                return carry
            lax.fori_loop(0, 12, body, 0)

    def build_bt(j):
        for s in range(2):
            t = jnp.transpose(bf[s, j])
            rows = pl.ds(pl.multiple_of(j * 384, 384), 384)
            bt[s, rows, :] = wide(t)

    def store_x(s, j, value):
        rows = pl.ds(pl.multiple_of(j * 384, 384), 384)
        xs[s, rows, :] = wide(value)

    def apply(m, s):
        return quad(mm(am[m, s], xs[s]), 384)

    def coarse_copies(it):
        q = {}
        g = rhs.at[it]
        first = counter[0]
        q["a1"] = [remote(g.at[z, y, 0], g.at[z, y, 0], yat(k), False) for k in (2, 1, 3)]
        q["f0"] = []

        def relay0(zz, h, dev):
            b = g.at[zz, pl.ds(2 * h, 2), 0]
            return remote(b, b, dev, False)

        q["p"] = {}
        q["m"] = {}
        for k in range(1, 5):
            for h in range(2):
                if k < 4 or h == 0:
                    q["p"][k, h] = relay0(lax.rem(z + 8 - (k - 1), 8), h, zat(1))
                if k < 4 or h == 1:
                    q["m"][k, h] = relay0(lax.rem(z + k - 1, 8), h, zat(7))
        zero_used = list(range(first, counter[0]))
        last0 = counter[0]
        counter[0] = first
        q["b1"] = [remote(g.at[z, y, 1], g.at[z, y, 1], zat(k), False) for k in (4, 3, 5, 2, 6, 1, 7)]

        def relay1(yy, h, dev):
            b = g.at[pl.ds(4 * h, 4), yy, 1]
            return remote(b, b, dev, False)

        q["u"] = {}
        q["v"] = {}
        for k in range(1, 3):
            for h in range(2):
                if k < 2 or h == 0:
                    q["u"][k, h] = relay1(lax.rem(y + 4 - (k - 1), 4), h, yat(1))
                if k < 2 or h == 1:
                    q["v"][k, h] = relay1(lax.rem(y + k - 1, 4), h, yat(3))
        counter[0] = max(last0, counter[0])

        def chip0(zz, lo, n):
            b = g.at[zz, pl.ds(lo, n), 0]
            return remote(b, b, sib, False)

        def chip1(lo, n, yy):
            b = g.at[pl.ds(lo, n), yy, 1]
            return remote(b, b, sib, False)

        q["f0own"] = chip0(z, 0, 4)
        q["f0p"] = {}
        q["f0m"] = {}
        for k in range(1, 5):
            for h in range(2):
                if k < 4 or h == 0:
                    q["f0p"][k, h] = chip0(lax.rem(z + 8 - k, 8), 2 * h, 2)
                if k < 4 or h == 1:
                    q["f0m"][k, h] = chip0(lax.rem(z + k, 8), 2 * h, 2)
        q["f1own"] = chip1(0, 8, y)
        q["f1u"] = {}
        q["f1v"] = {}
        for k in range(1, 3):
            for h in range(2):
                if k < 2 or h == 0:
                    q["f1u"][k, h] = chip1(4 * h, 4, lax.rem(y + 4 - k, 4))
                if k < 2 or h == 1:
                    q["f1v"][k, h] = chip1(4 * h, 4, lax.rem(y + k, 4))
        q["c0"] = q["a1"] + list(q["p"].values()) + list(q["m"].values()) + [q["f0own"]] + list(q["f0p"].values()) + list(q["f0m"].values())
        q["c1"] = q["b1"] + list(q["u"].values()) + list(q["v"].values()) + [q["f1own"]] + list(q["f1u"].values()) + list(q["f1v"].values())
        q["in0"] = [q["f0own"]] + list(q["f0p"].values()) + list(q["f0m"].values())
        q["in1"] = [q["f1own"]] + list(q["f1u"].values()) + list(q["f1v"].values())
        return q

    def coarse_step(q, n):
        @pl.when(co == 0)
        def _():
            if n == 0:
                for c in q["a1"]:
                    c.start()
            if n == 1:
                for c in q["a1"]:
                    c.wait_recv()
                for h in range(2):
                    q["p"][1, h].start()
                    q["m"][1, h].start()
                q["f0own"].start()
            if 2 <= n <= 5:
                k = n - 1
                for h in range(2):
                    for a, f in (("p", "f0p"), ("m", "f0m")):
                        if (k, h) in q[a]:
                            q[a][k, h].wait_recv()
                            if (k + 1, h) in q[a]:
                                q[a][k + 1, h].start()
                            q[f][k, h].start()
            if n == 5:
                for c in q["in1"]:
                    c.wait_recv()

        @pl.when(co == 1)
        def _():
            if n == 0:
                for c in q["b1"]:
                    c.start()
            if n == 2:
                for c in q["b1"]:
                    c.wait_recv()
                for h in range(2):
                    q["u"][1, h].start()
                    q["v"][1, h].start()
                q["f1own"].start()
            if 4 <= n <= 5:
                k = n - 3
                for h in range(2):
                    for a, f in (("u", "f1u"), ("v", "f1v")):
                        if (k, h) in q[a]:
                            q[a][k, h].wait_recv()
                            if (k + 1, h) in q[a]:
                                q[a][k + 1, h].start()
                            q[f][k, h].start()
            if n == 5:
                for c in q["in0"]:
                    c.wait_recv()

    def coarse_drain(q):
        @pl.when(co == 0)
        def _():
            for c in q["c0"]:
                c.wait_send()

        @pl.when(co == 1)
        def _():
            for c in q["c1"]:
                c.wait_send()

    def gather_copies(buf):
        g = {"own": [], "opp": [], "fwd": []}
        for s in range(2):
            g["own"].append(remote(buf.at[s, cr], buf.at[s, cr], sib))
            g["opp"].append(remote(buf.at[s, cr], buf.at[s, cr], opp))
            g["fwd"].append(remote(buf.at[s, oc], buf.at[s, oc], sib))
        return g

    def forward(g, s):
        g["opp"][s].wait_recv()
        g["fwd"][s].start()

    def arrived(g, s):
        g["own"][s].wait_recv()
        g["fwd"][s].wait_recv()

    def partial_restrict(it, own):
        for s in range(2):
            part[it, s] = quad(mm(bo[s], wide(own(s))), 96)
        c = remote(part.at[it, 1 - co], pin.at[it], sib)
        c.start()
        c.wait_recv()
        psend[it] = part[it, co] + pin[it]
        c2 = remote(psend.at[it], precv.at[it], opp)
        c2.start()
        return c2

    def coarse_solve(it):
        def body(i, acc):
            x = rhs[it, i].reshape(768, 128)
            cols = pl.ds(pl.multiple_of(i * 768, 768), 768)
            return acc + mm(km[:, cols], wide(x))
        acc = lax.fori_loop(0, 8, body, jnp.zeros((96, 256), f32))
        co48[it, cr] = quad(acc, 48)
        cs = [remote(co48.at[it, cr], co48.at[it, cr], dev) for dev in (opp, ops, sib)]
        for c in cs:
            c.start()
        return cs

    def rebuild(it, s):
        coarse = co48[it].reshape(2, 96, 128)[s]
        hi, lo = split(coarse)
        zero = jnp.zeros((32, 128), bf16)
        left = jnp.concatenate([hi, zero, hi, zero], axis=0)
        right = jnp.concatenate([lo, zero, jnp.zeros((128, 128), bf16)], axis=0)
        w = jnp.concatenate([left, right], axis=1)

        def body(j, carry):
            rows = pl.ds(pl.multiple_of(j * 384, 384), 384)
            v = lb[it, s, j] + halves(mm(bt[s, rows, :], w))
            xs[s, rows, :] = wide(v)
            return carry
        lax.fori_loop(0, 4, body, 0)
        rows = pl.ds(pl.multiple_of(cr * 384, 384), 384)
        v = lb[it, s, cr] + halves(mm(bt[s, rows, :], w))
        if it == 0:
            vsum[s] = v
        else:
            sol[s] = damping * (vsum[s] + v)

    def pick(m, s):
        return halves(mm(pickm[m], xs[s]))

    c_list_dn = remote(lists.at[co, pl.ds(0, 2)], rl.at[0], dn)
    c_list_up = remote(lists.at[co, pl.ds(2, 2)], rl.at[1], up)
    ld_b.wait()
    c_b1 = remote(bf.at[1 - cc, cr, pl.ds(0, 96)], bf.at[1 - cc, cr, pl.ds(0, 96)], otwin)
    c_b2 = remote(bf.at[cc, oc, pl.ds(0, 96)], bf.at[cc, oc, pl.ds(0, 96)], twin)
    c_bs = remote(bf.at[:, cr, pl.ds(0, 96)], bf.at[:, cr, pl.ds(0, 96)], sib)
    c_bo = remote(bf.at[:, oc, pl.ds(0, 96)], bf.at[:, oc, pl.ds(0, 96)], sib)
    c_b1.start()
    c_list_dn.start()
    c_list_up.start()
    for s in range(2):
        hi, lo = split(bf[s, cr, 0:96, :])
        bo[s, 0:96] = hi
        bo[s, 96:192] = lo
    ld_r.wait()
    gr = gather_copies(rb.at[0])
    c_part = partial_restrict(0, lambda s: rb[0, s, cr])
    for s in range(2):
        gr["opp"][s].start()
        gr["own"][s].start()
    c_bs.start()

    def zero_pad(j, carry):
        for s in range(2):
            bf[s, j, 96:128, :] = jnp.zeros((32, 384), f32)
        return carry
    lax.fori_loop(0, 4, zero_pad, 0)
    ld_l[0].wait()
    conv_matrix(0, 0)
    ld_s0 = load(6, s_hbm.at[0], stage.at[0])

    c_part.wait_recv()
    rhs[0, z, y, co] = psend[0] + precv[0]
    q = coarse_copies(0)
    coarse_step(q, 0)
    c_b1.wait_recv()
    c_b2.start()
    ld_l[1].wait()
    conv_matrix(0, 1)
    ld_s1 = load(7, s_hbm.at[1], stage.at[1])
    c_list_dn.wait_recv()
    c_list_up.wait_recv()
    coarse_step(q, 1)
    build_pick(0, lambda k: rl[0, 0, pl.ds(k, 1), :])
    coarse_step(q, 2)
    forward(gr, 0)
    build_pick(1, lambda k: rl[1, 0, pl.ds(k, 1), :])
    ld_k.wait()
    hi, lo = split(kst[...])
    km[0:48] = hi
    km[48:96] = lo
    coarse_step(q, 3)
    gl = gather_copies(lb.at[0])
    arrived(gr, 0)
    for j in range(4):
        store_x(0, j, rb[0, 0, j])
    lb[0, 0, cr] = apply(0, 0)
    gl["opp"][0].start()
    gl["own"][0].start()
    c_b2.wait_recv()
    c_bo.start()
    coarse_step(q, 4)
    forward(gr, 1)
    build_pick(2, lambda k: rl[co, 1, pl.ds(k, 1), :])
    arrived(gr, 1)
    for j in range(4):
        store_x(1, j, rb[0, 1, j])
    lb[0, 1, cr] = apply(0, 1)
    gl["opp"][1].start()
    gl["own"][1].start()
    coarse_step(q, 5)
    cs = coarse_solve(0)
    c_bs.wait_recv()
    c_bo.wait_recv()
    lax.fori_loop(0, 4, lambda j, carry: (build_bt(j), carry)[1], 0)
    forward(gl, 0)
    ld_s0.wait()
    conv_matrix(1, 0)
    ld_s1.wait()
    conv_matrix(1, 1)
    build_pick(3, lambda k: lists[co, 4, pl.ds(k, 1), :])
    build_scatter(0)
    build_scatter(1)
    ld_c.wait()
    for k in range(6):
        hi, lo = split(cst[k])
        cm[k, 0:128] = hi
        cm[k, 128:256] = lo

    for it in range(ITERS):
        for c in cs:
            c.wait_recv()
        arrived(gl, 0)
        rebuild(it, 0)
        ps[it, 1] = pick(1, 0)
        forward(gl, 1)
        arrived(gl, 1)
        rebuild(it, 1)
        ps[it, 0] = pick(0, 1)
        ps[it, co] = ps[it, co] + pick(2, co)
        c_up = remote(ps.at[it, 0], fr.at[it, 0], up)
        c_dn = remote(ps.at[it, 1], fr.at[it, 1], dn)
        c_up.start()
        c_dn.start()
        if it == 0:
            gy = gather_copies(rb.at[1])
        for s in range(2):
            if it == 0:
                rb[1, s, cr] = rb[0, s, cr] - damping * apply(1, s)
                gy["opp"][s].start()
                gy["own"][s].start()
            else:
                res[s] = r1[s] - damping * apply(1, s)
        own_rows = pick(3, 1 - co)
        if it == 0:
            forward(gy, 0)
        c_up.wait_recv()
        c_dn.wait_recv()
        src = own_rows + fr[it, 0] + fr[it, 1]
        for k in range(6):
            rows = slice(128 * k, 128 * (k + 1))
            tm[it, co, rows, :] = quad(mm(cm[k], wide(src[rows])), 128)
        c_tm = remote(tm.at[it, co], tm.at[it, co], sib)
        c_tm.start()
        if it == 0:
            forward(gy, 1)
        c_tm.wait_recv()
        tx = [wide(tm[it, s]) for s in range(2)]
        own = pl.ds(pl.multiple_of(cr * 384, 384), 384)
        for s in range(2):
            own_inflow = halves(mm(tt[s, own, :], tx[s]))
            if it == 0:
                r1[s] = rb[1, s, cr] + damping * own_inflow
                store_x(s, cr, r1[s])
            else:
                res[s] = res[s] + damping * own_inflow
        if it == 0:
            coarse_drain(q)
            c_part = partial_restrict(1, lambda s: r1[s])
            gl = gather_copies(lb.at[1])

            def fill(s):
                arrived(gy, s)

                def body(i, carry):
                    j = lax.rem(cr + i, 4)
                    rows = pl.ds(pl.multiple_of(j * 384, 384), 384)
                    v = rb[1, s, j] + damping * halves(mm(tt[s, rows, :], wide(tm[0, s])))
                    xs[s, rows, :] = wide(v)
                    return carry
                lax.fori_loop(1, 4, body, 0)

            fill(0)
            c_part.wait_recv()
            rhs[1, z, y, co] = psend[1] + precv[1]
            q = coarse_copies(1)
            coarse_step(q, 0)
            fill(1)
            lb[1, 0, cr] = apply(0, 0)
            gl["opp"][0].start()
            gl["own"][0].start()
            coarse_step(q, 1)
            lb[1, 1, cr] = apply(0, 1)
            gl["opp"][1].start()
            gl["own"][1].start()
            coarse_step(q, 2)
            coarse_step(q, 3)
            forward(gl, 0)
            coarse_step(q, 4)
            coarse_step(q, 5)
            cs = coarse_solve(1)
    coarse_drain(q)
    for c in pending:
        c.wait_send()


N_COPIES = 168


def per_device(
    load_cases,
    stiffness,
    local_inverse,
    coarse_basis,
    coarse_inverse,
    coupling,
    target_local_rows,
    neighbour_read_rows,
    neighbour,
    counts,
):
    d2 = lax.axis_index(SUB) * 2
    active = jnp.arange(6, dtype=jnp.int32)[None, :] < counts[:, None]
    near = jnp.where(active, neighbour, -9) - d2
    wanted = jnp.stack(
        [
            jnp.full((2,), -1, jnp.int32),
            jnp.full((2,), -2, jnp.int32),
            jnp.full((2,), 2, jnp.int32),
            jnp.full((2,), 3, jnp.int32),
            jnp.array([1, 0], jnp.int32),
        ],
        axis=1,
    )
    hit = (near[:, None, :] == wanted[:, :, None]) & active[:, None, :]
    lists = jnp.where(hit[:, :, :, None], neighbour_read_rows[:, None], -1)
    lists = jnp.pad(lists, ((0, 0), (0, 0), (0, 2), (0, 0)), constant_values=-1)
    any_spec = pl.BlockSpec(memory_space=pl.ANY)
    vmem = pl.BlockSpec(memory_space=pltpu.VMEM)
    block = jax.ShapeDtypeStruct((2, 384, 128), f32)
    V = pltpu.VMEM
    return pl.pallas_call(
        kernel,
        name="schwarz",
        out_shape=(block, block),
        in_specs=[any_spec] * 6 + [vmem] * 2,
        out_specs=(vmem, vmem),
        scratch_shapes=[
            V((2, 2, 4, 384, 128), f32),
            V((2, 2, 4, 384, 128), f32),
            V((2, 4, 128, 384), f32),
            V((2, 1536, 256), bf16),
            V((2, 192, 384), bf16),
            V((2, 2, 768, 1536), bf16),
            V((2, 384, 1536), f32),
            V((48, 6144), f32),
            V((96, 6144), bf16),
            V((2, 8, 4, 2, 96, 128), f32),
            V((2, 1536, 256), bf16),
            V((2, 384, 128), f32),
            V((2, 2, 96, 128), f32),
            V((2, 96, 128), f32),
            V((2, 96, 128), f32),
            V((2, 96, 128), f32),
            V((4, 768, 1536), bf16),
            V((2, 1536, 768), bf16),
            V((2, 2, 768, 128), f32),
            V((2, 2, 768, 128), f32),
            V((2, 2, 768, 128), f32),
            V((6, 128, 128), f32),
            V((6, 256, 128), bf16),
            V((2, 2, 8, 128), jnp.int32),
            V((2, 4, 48, 128), f32),
            V((2, 384, 128), f32),
            pltpu.SemaphoreType.DMA((8,)),
            pltpu.SemaphoreType.DMA((N_COPIES,)),
            pltpu.SemaphoreType.DMA((N_COPIES,)),
        ],
        compiler_params=pltpu.CompilerParams(
            collective_id=0, has_side_effects=True, vmem_limit_bytes=66_000_000
        ),
    )(
        load_cases, stiffness, local_inverse, coarse_basis, coarse_inverse, coupling,
        lists, target_local_rows,
    )


def solution(mesh):
    finer = Mesh(
        mesh.devices.reshape(8, 4, mesh.shape["crow"], mesh.shape["ccol"]),
        ("sub_0", "sub_1", "crow", "ccol"),
    )
    placed = (
        P(SUB, "crow", "ccol"),
        P(SUB, "crow", None),
        P(SUB, "crow", None),
        P(SUB, None, "crow"),
        P(SUB_CROW, None),
        P(SUB, None, None, None),
        P(SUB, None, None),
        P(SUB, None, None),
        P(SUB, None),
        P(SUB),
    )
    return jax.shard_map(
        per_device,
        mesh=finer,
        in_specs=placed,
        out_specs=(P(SUB, "crow", "ccol"), P(SUB, "crow", "ccol")),
        check_vma=False,
    )
```

time: 406 us -> 134 us (0.33)
  Pallas kernels: 0 us -> 125 us
  waiting for transfers between devices: 90.2 us -> 0 us
  blocking collectives: 86.7 us -> 0 us
  other arithmetic: 60.8 us -> 2.31 us
  matrix products: 53 us -> 0 us
  starting transfers between devices: 45.7 us -> 0 us
  local copies, waits for them, and re-layouts: 43.3 us -> 6.14 us
  between operations: 14.6 us -> 0.66 us
  loops' own time: 8.53 us -> 0 us
    pallas_call x0 -> x1, Pallas kernels: none -> 125 us  [per_device(): pl.pallas_call(kernel, name='schwarz', out_shape=(block, block), in_specs...]
    all_to_all x3 -> x0, blocking collectives: 63.2 us -> none  [sent_to_all(): return lax.all_to_all(copies, axis, split_axis=0, concat_axis=0, tiled=True)]
    dot_general x22 -> x0, matrix products: 53 us -> none  [the longest x12 14.8 us: add_slot(): jnp.einsum('snm,smc->snc', coupling[:, slot_index], sources, precision=hi...]
    all_to_all x5 -> x0, waiting for transfers between devices: 39 us -> none  [sent_to_all(): return lax.all_to_all(copies, axis, split_axis=0, concat_axis=0, tiled=True)]
    all_to_all x5 -> x0, starting transfers between devices: 31.2 us -> none  [sent_to_all(): return lax.all_to_all(copies, axis, split_axis=0, concat_axis=0, tiled=True)]
    scatter-add x12 -> x0, other arithmetic: 30.2 us -> none  [add_slot(): return inflow.at[target_rows].add(slot_terms * active_flag[:, None, None])]
    all_gather x2 -> x0, waiting for transfers between devices: 27.4 us -> none  [whole_of(): result = lax.all_gather(result, axes[number], axis=dim, tiled=True)]
    ppermute x6 -> x0, waiting for transfers between devices: 23.7 us -> none  [the longest x4 23.7 us: from_behind(): return lax.ppermute(block, axis, route)]
  transfers between devices with their start and end apart: 13 -> 0, of which waited for: 9 -> 0; matrix products, arithmetic and copies ran while one was open for 10% -> 0% of each run, Pallas kernels for 0% -> 0%
where the time goes in v1:
time: 134 us
  Pallas kernels  125 us (93%)
  local copies, waits for them, and re-layouts  6.14 us (5%)
  other arithmetic  2.31 us (2%)
    pallas_call x1, Pallas kernels, per_device(): pl.pallas_call(kernel, name='schwarz', out_shape=(block, block), in_specs...  125 us
    unnamed x4, local copies, waits for them, and re-layouts  5.52 us

profile of v1, /device:TPU:1, one launch (start us, length us, event | category | flops | bytes accessed | tf_op | source)
XLA Modules:
  0.0 134.1 jit_solution(10549525163060838229)
XLA Ops:
  0.6 0.8 select_subtract_fusion
  1.4 0.7 iota_compare_fusion
  2.1 0.8 compare_and_fusion
  2.9 1.3 copy.14.targets
  4.2 0.7 copy.13
  4.9 0.1 broadcast_select_fusion
  4.9 0.6 pad.4.lists
  5.6 125.0 %schwarz.1 = (f32[2,384,128]{2,1,0:T(8,128)}, f32[2,384,128]{2,1,0:T(8,128)}) custom-call(f32[2,384,128]{2,1,0:T(8,128)} %r_hbm.1, f32[2,384,1536]{2,1,0:T(8,128)} %s_hbm.1, f32[2,384,1536]{2,1,0:T(8,128)} %l_hbm.1, f32[2,96,384]{2,1,0:T(8,128)} %b_hbm.1, f32[48,6144]{1,0:T(8,128)} %k_hbm.1, f32[2,6,128,128]{3,2,1,0:T(8,128)} %c_hbm.1, ...), custom_call_target="tpu_custom_call" | custom-call | tf_op jit(solution)/shard_map/schwarz/pallas_call | solution.py:570
  130.6 1.8 %copy.17 = f32[2,384,128]{2,1,0:T(8,128)} copy(f32[2,384,128]{2,1,0:T(8,128)} %get-tuple-element.4) | data formatting | bytes 786432
  132.4 1.8 %copy.18 = f32[2,384,128]{2,1,0:T(8,128)} copy(f32[2,384,128]{2,1,0:T(8,128)} %get-tuple-element.5) | data formatting | bytes 786432

commit v2 on v1

v2 whole, which is shorter than its diff:
```python
import jax
import jax.numpy as jnp
from jax import lax
from jax.experimental import pallas as pl
from jax.experimental.pallas import tpu as pltpu
from jax.sharding import Mesh
from jax.sharding import PartitionSpec as P

ITERS = 2
SUB = ("sub_0", "sub_1")
SUB_CROW = ("sub_0", "sub_1", "crow")
AXES = ("sub_0", "sub_1", "crow", "ccol")

damping = 0.7
f32 = jnp.float32
bf16 = jnp.bfloat16


def split(x):
    hi = x.astype(bf16)
    lo = (x - hi.astype(f32)).astype(bf16)
    return hi, lo


def wide(x):
    hi, lo = split(x)
    return jnp.concatenate([hi, lo], axis=1)


def mm(a, b):
    return jnp.dot(a, b, preferred_element_type=f32)


def quad(acc, rows):
    return acc[:rows, :128] + acc[:rows, 128:] + acc[rows:, :128]


def halves(acc):
    return acc[:, :128] + acc[:, 128:]


def kernel(
    r_hbm, s_hbm, l_hbm, b_hbm, k_hbm, c_hbm, t_hbm, rows_hbm, nbr_hbm, cnt_hbm,
    out,
    rb, lb, bf, bt, bo, bw, am, stage, kst, km, rhs, xs, r1, part, pin, psend, precv,
    pickm, qm, tt, ps, fr, tm, cst, cm, rl, co48, vsum, res,
    targets, read_rows, nbr, cnt, lists,
    ldsem, ss, rs,
):
    z, y, cr, cc = [lax.axis_index(a) for a in AXES]
    co = lax.rem(cr, 2)
    oc = lax.rem(cr + 2, 4)
    sc = cr + 1 - 2 * co
    osc = lax.rem(sc + 2, 4)
    d = z * 4 + y
    d_up = lax.rem(d + 1, 32)
    d_dn = lax.rem(d + 31, 32)
    sib = (z, y, sc, cc)
    opp = (z, y, oc, cc)
    ops = (z, y, osc, cc)
    twin = (z, y, cr, 1 - cc)
    otwin = (z, y, oc, 1 - cc)
    up = (lax.div(d_up, 4), lax.rem(d_up, 4), cr, cc)
    dn = (lax.div(d_dn, 4), lax.rem(d_dn, 4), cr, cc)

    def yat(k):
        return (z, lax.rem(y + k, 4), cr, cc)

    def zat(k):
        return (lax.rem(z + k, 8), y, cr, cc)

    counter = [0]
    pending = []

    def remote(src, dst, dev, keep=True):
        i = counter[0]
        counter[0] += 1
        c = pltpu.make_async_remote_copy(
            src_ref=src, dst_ref=dst, send_sem=ss.at[i], recv_sem=rs.at[i],
            device_id=dev, device_id_type=pl.DeviceIdType.MESH,
        )
        if keep:
            pending.append(c)
        return c

    def load(i, src, dst):
        c = pltpu.make_async_copy(src, dst, ldsem.at[i])
        c.start()
        return c

    ld_b = load(0, b_hbm, bf.at[:, cr, pl.ds(0, 96)])
    ld_r = load(1, r_hbm, rb.at[0, :, cr])
    ld_i = [
        load(8, t_hbm, targets),
        load(9, rows_hbm, read_rows),
        load(10, nbr_hbm, nbr),
        load(11, cnt_hbm, cnt),
    ]
    ld_l = [load(2 + s, l_hbm.at[s], stage.at[s]) for s in range(2)]
    ld_k = load(4, k_hbm, kst)
    ld_c = load(5, c_hbm.at[co], cst)

    bar = pltpu.get_barrier_semaphore()

    def greet(devs):
        for dev in devs:
            pl.semaphore_signal(bar, inc=1, device_id=dev, device_id_type=pl.DeviceIdType.MESH)

    greet([sib, opp, ops, twin, otwin, up, dn])

    @pl.when(co == 0)
    def _():
        greet([yat(1), yat(2), yat(3), zat(1), zat(7)])

    @pl.when(co == 1)
    def _():
        greet([zat(1), zat(7), yat(1), yat(3)])

    def conv_matrix(m, s):
        def body(i, carry):
            rows = pl.ds(pl.multiple_of(i * 32, 32), 32)
            rows2 = pl.ds(pl.multiple_of(384 + i * 32, 32), 32)
            hi, lo = split(stage[s, rows, :])
            am[m, s, rows, :] = hi
            am[m, s, rows2, :] = lo
            return carry
        lax.fori_loop(0, 12, body, 0)

    lane = lax.broadcasted_iota(jnp.int32, (128, 128), 1)
    sub_iota = lax.broadcasted_iota(jnp.int32, (128, 128), 0)

    def build_pick(m, row_of):
        def body(k, carry):
            row = jnp.broadcast_to(row_of(k), (128, 128))
            col = jnp.transpose(row)
            rows = pl.ds(pl.multiple_of(k * 128, 128), 128)
            for t in range(12):
                pickm[m, rows, 128 * t:128 * (t + 1)] = jnp.where(
                    col == lane + 128 * t, 1.0, 0.0
                ).astype(bf16)
            return carry
        lax.fori_loop(0, 6, body, 0)

    def build_scatter(s):
        for k in range(6):
            row = jnp.broadcast_to(targets[k, s:s + 1, :], (128, 128))

            def body(t, carry):
                rows = pl.ds(pl.multiple_of(t * 128, 128), 128)
                tt[s, rows, 128 * k:128 * (k + 1)] = jnp.where(
                    row == sub_iota + 128 * t, 1.0, 0.0
                ).astype(bf16)
                return carry
            lax.fori_loop(0, 12, body, 0)

    def build_bt(j):
        for s in range(2):
            t = jnp.transpose(bf[s, j])
            rows = pl.ds(pl.multiple_of(j * 384, 384), 384)
            bt[s, rows, :] = wide(t)

    def store_x(s, j, value):
        rows = pl.ds(pl.multiple_of(j * 384, 384), 384)
        xs[s, rows, :] = wide(value)

    def apply(m, s):
        return quad(mm(am[m, s], xs[s]), 384)

    def coarse_copies(it):
        q = {}
        g = rhs.at[it]
        first = counter[0]

        def block(zz, yy, half, dev):
            b = g.at[zz, yy, half]
            return remote(b, b, dev, False)

        def zm(k):
            return lax.rem(z + 8 + k, 8)

        def ym(k):
            return lax.rem(y + 4 + k, 4)

        for k in (1, 3, 2):
            q["y", k] = block(z, y, 0, yat(k))
        for j in range(4):
            for h in range(1, 5):
                if h < 4 or j < 2:
                    q["p", j, h] = block(zm(1 - h), ym(-j), 0, zat(1))
                if h < 4 or j >= 2:
                    q["m", j, h] = block(zm(h - 1), ym(-j), 0, zat(7))
        keys0 = list(q)
        last = counter[0]
        counter[0] = first
        for h in range(1, 5):
            q["s", h] = block(zm(1 - h), y, 1, zat(1))
            if h < 4:
                q["t", h] = block(zm(h - 1), y, 1, zat(7))
        for k in range(8):
            for h in range(1, 3):
                if h < 2 or k % 2 == 0:
                    q["u", k, h] = block(zm(-k), ym(1 - h), 1, yat(1))
                if h < 2 or k % 2 == 1:
                    q["v", k, h] = block(zm(-k), ym(h - 1), 1, yat(3))
        keys1 = [k for k in q if k not in keys0]
        counter[0] = max(last, counter[0])
        q["c0"] = [q[k] for k in keys0]
        q["c1"] = [q[k] for k in keys1]
        f0 = {}
        f0["y", 0] = block(z, y, 0, sib)
        for k in (1, 2, 3):
            f0["y", k] = block(z, ym(-k), 0, sib)
        for key in keys0:
            if key[0] == "p":
                f0[key] = block(zm(-key[2]), ym(-key[1]), 0, sib)
            if key[0] == "m":
                f0[key] = block(zm(key[2]), ym(-key[1]), 0, sib)
        f1 = {}
        f1["z", 0] = block(z, y, 1, sib)
        for k in range(1, 8):
            f1["z", k] = block(zm(-k), y, 1, sib)
        for key in keys1:
            if key[0] == "u":
                f1[key] = block(zm(-key[1]), ym(-key[2]), 1, sib)
            if key[0] == "v":
                f1[key] = block(zm(-key[1]), ym(key[2]), 1, sib)
        q["f0"] = f0
        q["f1"] = f1
        q["c0"] = q["c0"] + list(f0.values())
        q["c1"] = q["c1"] + list(f1.values())
        return q

    def coarse_step(q, n):
        def relay(f, a, b, j, hops):
            for h in hops:
                for way in (a, b):
                    if (way, j, h) in q:
                        q[way, j, h].wait_recv()
                        if (way, j, h + 1) in q:
                            q[way, j, h + 1].start()
                        f[way, j, h].start()

        @pl.when(co == 0)
        def _():
            f = q["f0"]

            def enter(k):
                q["y", k].wait_recv()
                q["p", k, 1].start()
                q["m", k, 1].start()
                f["y", k].start()

            if n == 0:
                for k in (1, 3, 2):
                    q["y", k].start()
                q["p", 0, 1].start()
                q["m", 0, 1].start()
                f["y", 0].start()
            if n == 1:
                relay(f, "p", "m", 0, [1])
                enter(1)
                enter(3)
            if n == 2:
                enter(2)
                relay(f, "p", "m", 0, [2])
            if 3 <= n <= 6:
                for j in (1, 3, 2):
                    relay(f, "p", "m", j, [n - 2])
                if n < 5:
                    relay(f, "p", "m", 0, [n])
            if n >= 7:
                for key, c in q["f1"].items():
                    if (key[1] == 4) == (n == 8):
                        c.wait_recv()

        @pl.when(co == 1)
        def _():
            f = q["f1"]

            def enter(h):
                for way, k in (("s", h), ("t", 8 - h)):
                    if (way, h) in q:
                        q[way, h].wait_recv()
                        if (way, h + 1) in q:
                            q[way, h + 1].start()
                        q["u", k, 1].start()
                        q["v", k, 1].start()
                        f["z", k].start()

            def both(h, hop):
                for k in sorted({h % 8, (8 - h) % 8}):
                    relay(f, "u", "v", k, [hop])

            if n == 0:
                q["s", 1].start()
                q["t", 1].start()
                q["u", 0, 1].start()
                q["v", 0, 1].start()
                f["z", 0].start()
            if 1 <= n <= 4:
                enter(n)
            if 1 <= n <= 5:
                both(n - 1, 1)
            if 2 <= n <= 6:
                both(n - 2, 2)
            if n >= 7:
                for key, c in q["f0"].items():
                    if (key[-1] == 4) == (n == 8):
                        c.wait_recv()

    def coarse_drain(q):
        @pl.when(co == 0)
        def _():
            for c in q["c0"]:
                c.wait_send()

        @pl.when(co == 1)
        def _():
            for c in q["c1"]:
                c.wait_send()

    def gather_copies(buf):
        g = {"own": [], "opp": [], "fwd": []}
        for s in range(2):
            g["own"].append(remote(buf.at[s, cr], buf.at[s, cr], sib))
            g["opp"].append(remote(buf.at[s, cr], buf.at[s, cr], opp))
            g["fwd"].append(remote(buf.at[s, oc], buf.at[s, oc], sib))
        return g

    def forward(g, s):
        g["opp"][s].wait_recv()
        g["fwd"][s].start()

    def arrived(g, s):
        g["own"][s].wait_recv()
        g["fwd"][s].wait_recv()

    def combine():
        c = remote(part.at[1 - co], pin, sib)
        c.start()
        c.wait_recv()
        psend[...] = part[co] + pin[...]
        c2 = remote(psend, precv, opp)
        c2.start()
        return c2

    def solve_group(it, off):
        i = lax.rem(z + off, 8)
        x = rhs[it, i].reshape(768, 128)
        cols = pl.ds(pl.multiple_of(i * 768, 768), 768)
        return mm(km[:, cols], wide(x))

    def solve_most(it):
        def body(i, acc):
            return acc + solve_group(it, i + lax.div(i, 4))
        return lax.fori_loop(0, 7, body, jnp.zeros((96, 256), f32))

    def solve_rest(it, acc):
        co48[it, cr] = quad(acc + solve_group(it, 4), 48)
        cs = [remote(co48.at[it, cr], co48.at[it, cr], dev) for dev in (opp, ops, sib)]
        for c in cs:
            c.start()
        return cs

    def weights(it, s):
        first = co48[it, pl.ds(2 * s, 2)].reshape(96, 128)
        hi, lo = split(first)
        zero = jnp.zeros((32, 128), bf16)
        left = jnp.concatenate([hi, zero, hi, zero], axis=0)
        right = jnp.concatenate([lo, zero, jnp.zeros((128, 128), bf16)], axis=0)
        return jnp.concatenate([left, right], axis=1)

    def rebuild(it, s):
        w = weights(it, s)

        def body(j, carry):
            rows = pl.ds(pl.multiple_of(j * 384, 384), 384)
            v = lb[it, s, j] + halves(mm(bt[s, rows, :], w))
            xs[s, rows, :] = wide(v)
            return carry
        lax.fori_loop(0, 4, body, 0)
        rows = pl.ds(pl.multiple_of(cr * 384, 384), 384)
        v = lb[it, s, cr] + halves(mm(bt[s, rows, :], w))
        if it == 0:
            vsum[s] = v
        else:
            out[0, s] = vsum[s] + v

    def pick(m, s, g):
        return halves(mm(pickm[m, 384 * g:384 * (g + 1)], xs[s]))

    ld_b.wait()
    for s in range(2):
        hi, lo = split(bf[s, cr, 0:96, :])
        bo[s, 0:96] = hi
        bo[s, 96:192] = lo
    ld_r.wait()
    for s in range(2):
        part[s] = quad(mm(bo[s], wide(rb[0, s, cr])), 96)
    for c in ld_i:
        c.wait()
    wanted = [-1, -2, 2, 3, 1 - co]
    for k in range(6):
        near = nbr[co, k] - 2 * d
        on = (cnt[co] > k).astype(jnp.int32)
        row = read_rows[k, pl.ds(co, 1), :]
        for a in range(5):
            h = (near == wanted[a]).astype(jnp.int32) * on
            lists[a, k:k + 1, :] = row * h + (h - 1)

    @pl.when(co == 0)
    def _():
        pl.semaphore_wait(bar, 12)

    @pl.when(co == 1)
    def _():
        pl.semaphore_wait(bar, 11)

    c_part = combine()
    c_list_dn = remote(lists.at[pl.ds(0, 2)], rl.at[0], dn)
    c_list_up = remote(lists.at[pl.ds(2, 2)], rl.at[1], up)
    c_b1 = remote(bf.at[1 - cc, cr, pl.ds(0, 96)], bf.at[1 - cc, cr, pl.ds(0, 96)], otwin)
    c_b2 = remote(bf.at[cc, oc, pl.ds(0, 96)], bf.at[cc, oc, pl.ds(0, 96)], twin)
    c_bs = remote(bf.at[:, cr, pl.ds(0, 96)], bf.at[:, cr, pl.ds(0, 96)], sib)
    c_bo = remote(bf.at[:, oc, pl.ds(0, 96)], bf.at[:, oc, pl.ds(0, 96)], sib)
    c_b1.start()
    gr = gather_copies(rb.at[0])
    for s in range(2):
        gr["opp"][s].start()
        gr["own"][s].start()
    c_list_dn.start()
    c_list_up.start()
    c_bs.start()

    def zero_pad(j, carry):
        for s in range(2):
            bf[s, j, 96:128, :] = jnp.zeros((32, 384), f32)
        return carry
    lax.fori_loop(0, 4, zero_pad, 0)
    ld_l[0].wait()
    conv_matrix(0, 0)
    ld_s0 = load(6, s_hbm.at[0], stage.at[0])
    ld_l[1].wait()
    conv_matrix(0, 1)
    ld_s1 = load(7, s_hbm.at[1], stage.at[1])

    c_part.wait_recv()
    rhs[0, z, y, co] = psend[...] + precv[...]
    q = coarse_copies(0)
    coarse_step(q, 0)
    ld_k.wait()
    hi, lo = split(kst[...])
    km[0:48] = hi
    km[48:96] = lo
    c_list_dn.wait_recv()
    c_list_up.wait_recv()
    build_pick(0, lambda k: rl[0, 0, pl.ds(k, 1), :])
    coarse_step(q, 1)
    build_pick(1, lambda k: rl[1, 0, pl.ds(k, 1), :])
    coarse_step(q, 2)
    forward(gr, 0)
    build_scatter(0)
    coarse_step(q, 3)
    gl = gather_copies(lb.at[0])
    arrived(gr, 0)
    for j in range(4):
        store_x(0, j, rb[0, 0, j])
    lb[0, 0, cr] = apply(0, 0)
    gl["opp"][0].start()
    gl["own"][0].start()
    coarse_step(q, 4)
    c_b1.wait_recv()
    c_b2.start()
    build_pick(2, lambda k: rl[co, 1, pl.ds(k, 1), :])
    coarse_step(q, 5)
    forward(gr, 1)
    arrived(gr, 1)
    for j in range(4):
        store_x(1, j, rb[0, 1, j])
    lb[0, 1, cr] = apply(0, 1)
    gl["opp"][1].start()
    gl["own"][1].start()
    coarse_step(q, 7)
    acc = solve_most(0)
    coarse_step(q, 6)
    coarse_step(q, 8)
    cs = solve_rest(0, acc)
    c_b2.wait_recv()
    c_bo.start()
    ld_s0.wait()
    conv_matrix(1, 0)
    ld_s1.wait()
    conv_matrix(1, 1)
    build_pick(3, lambda k: lists[4, pl.ds(k, 1), :])
    forward(gl, 0)
    build_scatter(1)
    c_bs.wait_recv()
    c_bo.wait_recv()
    lax.fori_loop(0, 4, lambda j, carry: (build_bt(j), carry)[1], 0)
    for j in range(4):
        hi, lo = split(bf[co, j, 0:96, :])
        bw[0:96, 384 * j:384 * (j + 1)] = hi
        bw[96:192, 384 * j:384 * (j + 1)] = lo
    ld_c.wait()
    for k in range(6):
        hi, lo = split(cst[k])
        cm[k, 0:128] = hi
        cm[k, 128:256] = lo

    for it in range(ITERS):
        c_up = []
        c_dn = []
        for g in range(2):
            part_rows = pl.ds(384 * g, 384)
            c_up.append(remote(ps.at[it, 0, part_rows], fr.at[it, 0, part_rows], up))
            c_dn.append(remote(ps.at[it, 1, part_rows], fr.at[it, 1, part_rows], dn))
        if it == 1:
            for s in range(2):
                arrived(gl, s)
                for j in range(4):
                    store_x(s, j, lb[1, s, j])
            for g in range(2):
                rows = slice(384 * g, 384 * (g + 1))
                ps[1, 1, rows] = pick(1, 0, g)
                ps[1, 0, rows] = pick(0, 1, g)
                ps[1, co, rows] = ps[1, co, rows] + pick(2, co, g)
            for c in cs:
                c.wait_recv()
            ws = [weights(1, 1), weights(1, 0), weights(1, co)]
            for g in range(2):
                rows = slice(384 * g, 384 * (g + 1))
                for m, dest in ((0, 0), (1, 1), (2, co)):
                    ps[1, dest, rows] = ps[1, dest, rows] + halves(mm(qm[m, rows], ws[m]))
                c_up[g].start()
                c_dn[g].start()
            rebuild(1, 0)
            rebuild(1, 1)
        if it == 0:
            for c in cs:
                c.wait_recv()
            arrived(gl, 0)
            rebuild(0, 0)
            for g in range(2):
                rows = slice(384 * g, 384 * (g + 1))
                ps[0, 1, rows] = pick(1, 0, g)

                @pl.when(co == 0)
                def _():
                    c_dn[g].start()
            forward(gl, 1)
            arrived(gl, 1)
            rebuild(0, 1)
            for g in range(2):
                rows = slice(384 * g, 384 * (g + 1))
                ps[0, 0, rows] = pick(0, 1, g)

                @pl.when(co == 1)
                def _():
                    c_up[g].start()
                ps[0, co, rows] = ps[0, co, rows] + pick(2, co, g)

                @pl.when(co == 0)
                def _():
                    c_up[g].start()

                @pl.when(co == 1)
                def _():
                    c_dn[g].start()
        if it == 0:
            gy = gather_copies(rb.at[1])
        for s in range(2):
            if it == 0:
                rb[1, s, cr] = rb[0, s, cr] - damping * apply(1, s)
                gy["opp"][s].start()
                gy["own"][s].start()
            else:
                res[s] = r1[s] - damping * apply(1, s)
        own_rows = [pick(3, 1 - co, g) for g in range(2)]
        c_tm = []
        for g in range(2):
            if it == 0:
                for m, src_s in ((0, 1), (1, 0)) if g == 0 else ((2, co),):
                    for h in range(2):
                        rows = slice(384 * h, 384 * (h + 1))
                        qm[m, rows] = mm(pickm[m, rows], bt[src_s]).astype(bf16)
            c_up[g].wait_recv()
            c_dn[g].wait_recv()
            part_rows = pl.ds(384 * g, 384)
            src = own_rows[g] + fr[it, 0, part_rows] + fr[it, 1, part_rows]
            for k in range(3):
                rows = slice(384 * g + 128 * k, 384 * g + 128 * (k + 1))
                tm[it, co, rows, :] = quad(
                    mm(cm[3 * g + k], wide(src[128 * k:128 * (k + 1)])), 128
                )
            c = remote(tm.at[it, co, part_rows], tm.at[it, co, part_rows], sib)
            c.start()
            c_tm.append(c)
            if it == 0:
                forward(gy, g)
        for c in c_tm:
            c.wait_recv()
        tx = [wide(tm[it, s]) for s in range(2)]
        own = pl.ds(pl.multiple_of(cr * 384, 384), 384)
        for s in range(2):
            own_inflow = halves(mm(tt[s, own, :], tx[s]))
            if it == 0:
                r1[s] = rb[1, s, cr] + damping * own_inflow
                store_x(s, cr, r1[s])
            else:
                out[1, s] = 0.5 * (res[s] + damping * own_inflow)
        if it == 0:
            coarse_drain(q)
            gl = gather_copies(lb.at[1])

            def fill(s):
                def body(i, carry):
                    j = lax.rem(cr + i, 4)
                    rows = pl.ds(pl.multiple_of(j * 384, 384), 384)
                    v = rb[1, s, j] + damping * halves(mm(tt[s, rows, :], wide(tm[0, s])))
                    xs[s, rows, :] = wide(v)
                    return carry
                lax.fori_loop(1, 4, body, 0)

            arrived(gy, 0)
            arrived(gy, 1)
            fill(co)
            rhs[1, z, y, co] = quad(mm(bw[...], xs[co]), 96)
            q = coarse_copies(1)
            coarse_step(q, 0)
            fill(1 - co)
            coarse_step(q, 1)
            lb[1, 0, cr] = apply(0, 0)
            gl["opp"][0].start()
            gl["own"][0].start()
            coarse_step(q, 2)
            lb[1, 1, cr] = apply(0, 1)
            gl["opp"][1].start()
            gl["own"][1].start()
            for n in range(3, 6):
                coarse_step(q, n)
            forward(gl, 0)
            coarse_step(q, 7)
            acc = solve_most(1)
            coarse_step(q, 6)
            forward(gl, 1)
            coarse_step(q, 8)
            cs = solve_rest(1, acc)
    coarse_drain(q)
    for c in pending:
        c.wait_send()


N_COPIES = 260


def per_device(
    load_cases,
    stiffness,
    local_inverse,
    coarse_basis,
    coarse_inverse,
    coupling,
    target_local_rows,
    neighbour_read_rows,
    neighbour,
    counts,
):
    any_spec = pl.BlockSpec(memory_space=pl.ANY)
    vmem = pl.BlockSpec(memory_space=pltpu.VMEM)
    V = pltpu.VMEM
    both = pl.pallas_call(
        kernel,
        name="schwarz",
        out_shape=jax.ShapeDtypeStruct((2, 2, 384, 128), f32),
        in_specs=[any_spec] * 10,
        out_specs=vmem,
        scratch_shapes=[
            V((2, 2, 4, 384, 128), f32),
            V((2, 2, 4, 384, 128), f32),
            V((2, 4, 128, 384), f32),
            V((2, 1536, 256), bf16),
            V((2, 192, 384), bf16),
            V((192, 1536), bf16),
            V((2, 2, 768, 1536), bf16),
            V((2, 384, 1536), f32),
            V((48, 6144), f32),
            V((96, 6144), bf16),
            V((2, 8, 4, 2, 96, 128), f32),
            V((2, 1536, 256), bf16),
            V((2, 384, 128), f32),
            V((2, 96, 128), f32),
            V((96, 128), f32),
            V((96, 128), f32),
            V((96, 128), f32),
            V((4, 768, 1536), bf16),
            V((3, 768, 256), bf16),
            V((2, 1536, 768), bf16),
            V((2, 2, 768, 128), f32),
            V((2, 2, 768, 128), f32),
            V((2, 2, 768, 128), f32),
            V((6, 128, 128), f32),
            V((6, 256, 128), bf16),
            V((2, 2, 8, 128), jnp.int32),
            V((2, 4, 48, 128), f32),
            V((2, 384, 128), f32),
            V((2, 384, 128), f32),
            V((6, 2, 128), jnp.int32),
            V((6, 2, 128), jnp.int32),
            pltpu.SMEM((2, 6), jnp.int32),
            pltpu.SMEM((2,), jnp.int32),
            V((5, 8, 128), jnp.int32),
            pltpu.SemaphoreType.DMA((12,)),
            pltpu.SemaphoreType.DMA((N_COPIES,)),
            pltpu.SemaphoreType.DMA((N_COPIES,)),
        ],
        compiler_params=pltpu.CompilerParams(
            collective_id=0, has_side_effects=True, vmem_limit_bytes=66_000_000
        ),
    )(
        load_cases, stiffness, local_inverse, coarse_basis, coarse_inverse, coupling,
        target_local_rows.transpose(1, 0, 2), neighbour_read_rows.transpose(1, 0, 2),
        neighbour, counts,
    )
    return damping * both[0], 2.0 * both[1]


def solution(mesh):
    finer = Mesh(
        mesh.devices.reshape(8, 4, mesh.shape["crow"], mesh.shape["ccol"]),
        ("sub_0", "sub_1", "crow", "ccol"),
    )
    placed = (
        P(SUB, "crow", "ccol"),
        P(SUB, "crow", None),
        P(SUB, "crow", None),
        P(SUB, None, "crow"),
        P(SUB_CROW, None),
        P(SUB, None, None, None),
        P(SUB, None, None),
        P(SUB, None, None),
        P(SUB, None),
        P(SUB),
    )
    return jax.shard_map(
        per_device,
        mesh=finer,
        in_specs=placed,
        out_specs=(P(SUB, "crow", "ccol"), P(SUB, "crow", "ccol")),
        check_vma=False,
    )
```

time: 134 us -> 113 us (0.84)
  Pallas kernels: 125 us -> 110 us
  local copies, waits for them, and re-layouts: 6.14 us -> 0 us
    pallas_call x1, Pallas kernels: 125 us -> 110 us  [per_device(): pl.pallas_call(kernel, name='schwarz', out_shape=jax.ShapeDtypeStruct((2,...]
    unnamed x4 -> x0, local copies, waits for them, and re-layouts: 5.52 us -> none
    mul x0 -> x1, other arithmetic: none -> 2.05 us  [per_device(): return (damping * both[0], 2.0 * both[1])]
where the time goes in v2:
time: 113 us; the launch traced here: 112 us
  Pallas kernels  110 us (97%)
  other arithmetic  2.05 us (2%)
    pallas_call x1, Pallas kernels, per_device(): pl.pallas_call(kernel, name='schwarz', out_shape=jax.ShapeDtypeStruct((2,...  110 us

profile of v2, /device:TPU:1, one launch (start us, length us, event | category | flops | bytes accessed | tf_op | source)
XLA Modules:
  0.0 112.4 jit_solution(14828199299012504022)
XLA Ops:
  0.6 109.7 %schwarz.1 = f32[2,2,384,128]{3,2,1,0:T(8,128)} custom-call(f32[2,384,128]{2,1,0:T(8,128)} %r_hbm.1, f32[2,384,1536]{2,1,0:T(8,128)} %s_hbm.1, f32[2,384,1536]{2,1,0:T(8,128)} %l_hbm.1, f32[2,96,384]{2,1,0:T(8,128)} %b_hbm.1, f32[48,6144]{1,0:T(8,128)} %k_hbm.1, f32[2,6,128,128]{3,2,1,0:T(8,128)} %c_hbm.1, s32[6,2,128]{2,1,0:T(2,128)} %bitcast.6, ...), custom_call_target="tpu_custom_call" | custom-call | tf_op jit(solution)/shard_map/schwarz/pallas_call | solution.py:671
  110.4 2.1 %multiply_bitcast_fusion = (f32[2,384,128]{2,1,0:T(8,128)}, f32[2,384,128]{2,1,0:T(8,128)}) fusion(f32[2,2,384,128]{3,2,1,0:T(8,128)} %schwarz.1), kind=kLoop, calls=%fused_computation | loop fusion | flops 196608 | bytes 1572864 | tf_op jit(solution)/shard_map/mul | solution.py:724

commit v3 on v2

--- a/solution.py
+++ b/solution.py
@@ -42,7 +42,7 @@
 def kernel(
     r_hbm, s_hbm, l_hbm, b_hbm, k_hbm, c_hbm, t_hbm, rows_hbm, nbr_hbm, cnt_hbm,
     out,
-    rb, lb, bf, bt, bo, bw, am, stage, kst, km, rhs, xs, r1, part, pin, psend, precv,
+    rb, lb, bf, bt, bo, bw, am, stage, kst, km, rhs, xs, r1, part, pin,
     pickm, qm, tt, ps, fr, tm, cst, cm, rl, co48, vsum, res,
     targets, read_rows, nbr, cnt, lists,
     ldsem, ss, rs,
@@ -319,30 +319,38 @@
             for c in q["c1"]:
                 c.wait_send()
 
-    def gather_copies(buf):
+    def gather_copies(buf, order=(0, 1)):
         g = {"own": [], "opp": [], "fwd": []}
-        for s in range(2):
+        for s in order:
             g["own"].append(remote(buf.at[s, cr], buf.at[s, cr], sib))
-            g["opp"].append(remote(buf.at[s, cr], buf.at[s, cr], opp))
+            g["opp"].append([])
+            for h in range(2):
+                b = buf.at[s, cr, pl.ds(192 * h, 192)]
+                g["opp"][-1].append(remote(b, b, opp))
             g["fwd"].append(remote(buf.at[s, oc], buf.at[s, oc], sib))
         return g
 
     def forward(g, s):
-        g["opp"][s].wait_recv()
+        for c in g["opp"][s]:
+            c.wait_recv()
         g["fwd"][s].start()
+
+    def send(g, s):
+        for c in g["opp"][s]:
+            c.start()
+        g["own"][s].start()
 
     def arrived(g, s):
         g["own"][s].wait_recv()
         g["fwd"][s].wait_recv()
 
     def combine():
-        c = remote(part.at[1 - co], pin, sib)
-        c.start()
-        c.wait_recv()
-        psend[...] = part[co] + pin[...]
-        c2 = remote(psend, precv, opp)
-        c2.start()
-        return c2
+        cs = []
+        for i, (half, dev) in enumerate(((1 - co, sib), (co, opp), (1 - co, ops))):
+            c = remote(part.at[half], pin.at[i], dev)
+            c.start()
+            cs.append(c)
+        return cs
 
     def solve_group(it, off):
         i = lax.rem(z + off, 8)
@@ -426,8 +434,7 @@
     c_b1.start()
     gr = gather_copies(rb.at[0])
     for s in range(2):
-        gr["opp"][s].start()
-        gr["own"][s].start()
+        send(gr, s)
     c_list_dn.start()
     c_list_up.start()
     c_bs.start()
@@ -444,8 +451,9 @@
     conv_matrix(0, 1)
     ld_s1 = load(7, s_hbm.at[1], stage.at[1])
 
-    c_part.wait_recv()
-    rhs[0, z, y, co] = psend[...] + precv[...]
+    for c in c_part:
+        c.wait_recv()
+    rhs[0, z, y, co] = (part[co] + pin[0]) + (pin[1] + pin[2])
     q = coarse_copies(0)
     coarse_step(q, 0)
     ld_k.wait()
@@ -466,33 +474,33 @@
     for j in range(4):
         store_x(0, j, rb[0, 0, j])
     lb[0, 0, cr] = apply(0, 0)
-    gl["opp"][0].start()
-    gl["own"][0].start()
+    send(gl, 0)
     coarse_step(q, 4)
     c_b1.wait_recv()
     c_b2.start()
     build_pick(2, lambda k: rl[co, 1, pl.ds(k, 1), :])
+    forward(gr, 1)
     coarse_step(q, 5)
-    forward(gr, 1)
     arrived(gr, 1)
     for j in range(4):
         store_x(1, j, rb[0, 1, j])
     lb[0, 1, cr] = apply(0, 1)
-    gl["opp"][1].start()
+    gl["opp"][1][0].start()
     gl["own"][1].start()
     coarse_step(q, 7)
     acc = solve_most(0)
     coarse_step(q, 6)
     coarse_step(q, 8)
     cs = solve_rest(0, acc)
-    c_b2.wait_recv()
-    c_bo.start()
+    gl["opp"][1][1].start()
     ld_s0.wait()
     conv_matrix(1, 0)
     ld_s1.wait()
     conv_matrix(1, 1)
     build_pick(3, lambda k: lists[4, pl.ds(k, 1), :])
     forward(gl, 0)
+    c_b2.wait_recv()
+    c_bo.start()
     build_scatter(1)
     c_bs.wait_recv()
     c_bo.wait_recv()
@@ -515,8 +523,9 @@
             c_up.append(remote(ps.at[it, 0, part_rows], fr.at[it, 0, part_rows], up))
             c_dn.append(remote(ps.at[it, 1, part_rows], fr.at[it, 1, part_rows], dn))
         if it == 1:
+            arrived(gl, 0)
+            arrived(gl, 1)
             for s in range(2):
-                arrived(gl, s)
                 for j in range(4):
                     store_x(s, j, lb[1, s, j])
             for g in range(2):
@@ -540,6 +549,7 @@
                 c.wait_recv()
             arrived(gl, 0)
             rebuild(0, 0)
+            forward(gl, 1)
             for g in range(2):
                 rows = slice(384 * g, 384 * (g + 1))
                 ps[0, 1, rows] = pick(1, 0, g)
@@ -547,9 +557,9 @@
                 @pl.when(co == 0)
                 def _():
                     c_dn[g].start()
-            forward(gl, 1)
             arrived(gl, 1)
             rebuild(0, 1)
+            gy = gather_copies(rb.at[1])
             for g in range(2):
                 rows = slice(384 * g, 384 * (g + 1))
                 ps[0, 0, rows] = pick(0, 1, g)
@@ -566,14 +576,10 @@
                 @pl.when(co == 1)
                 def _():
                     c_dn[g].start()
-        if it == 0:
-            gy = gather_copies(rb.at[1])
-        for s in range(2):
-            if it == 0:
-                rb[1, s, cr] = rb[0, s, cr] - damping * apply(1, s)
-                gy["opp"][s].start()
-                gy["own"][s].start()
-            else:
+                rb[1, g, cr] = rb[0, g, cr] - damping * apply(1, g)
+                send(gy, g)
+        if it == 1:
+            for s in range(2):
                 res[s] = r1[s] - damping * apply(1, s)
         own_rows = [pick(3, 1 - co, g) for g in range(2)]
         c_tm = []
@@ -610,7 +616,7 @@
                 out[1, s] = 0.5 * (res[s] + damping * own_inflow)
         if it == 0:
             coarse_drain(q)
-            gl = gather_copies(lb.at[1])
+            gl = gather_copies(lb.at[1], (co, 1 - co))
 
             def fill(s):
                 def body(i, carry):
@@ -627,15 +633,13 @@
             rhs[1, z, y, co] = quad(mm(bw[...], xs[co]), 96)
             q = coarse_copies(1)
             coarse_step(q, 0)
+            lb[1, co, cr] = apply(0, co)
+            send(gl, 0)
             fill(1 - co)
             coarse_step(q, 1)
-            lb[1, 0, cr] = apply(0, 0)
-            gl["opp"][0].start()
-            gl["own"][0].start()
+            lb[1, 1 - co, cr] = apply(0, 1 - co)
+            send(gl, 1)
             coarse_step(q, 2)
-            lb[1, 1, cr] = apply(0, 1)
-            gl["opp"][1].start()
-            gl["own"][1].start()
             for n in range(3, 6):
                 coarse_step(q, n)
             forward(gl, 0)
@@ -689,9 +693,7 @@
             V((2, 1536, 256), bf16),
             V((2, 384, 128), f32),
             V((2, 96, 128), f32),
-            V((96, 128), f32),
-            V((96, 128), f32),
-            V((96, 128), f32),
+            V((3, 96, 128), f32),
             V((4, 768, 1536), bf16),
             V((3, 768, 256), bf16),
             V((2, 1536, 768), bf16),

time: 113 us -> 108 us (0.956)
  Pallas kernels: 110 us -> 105 us
    pallas_call x1, Pallas kernels: 110 us -> 105 us  [per_device(): pl.pallas_call(kernel, name='schwarz', out_shape=jax.ShapeDtypeStruct((2,...]
where the time goes in v3:
time: 108 us
  Pallas kernels  105 us (97%)
  other arithmetic  2.05 us (2%)
    pallas_call x1, Pallas kernels, per_device(): pl.pallas_call(kernel, name='schwarz', out_shape=jax.ShapeDtypeStruct((2,...  105 us

profile of v3, /device:TPU:1, one launch (start us, length us, event | category | flops | bytes accessed | tf_op | source)
XLA Modules:
  0.0 108.1 jit_solution(4575813304258882904)
XLA Ops:
  0.6 105.4 %schwarz.1 = f32[2,2,384,128]{3,2,1,0:T(8,128)} custom-call(f32[2,384,128]{2,1,0:T(8,128)} %r_hbm.1, f32[2,384,1536]{2,1,0:T(8,128)} %s_hbm.1, f32[2,384,1536]{2,1,0:T(8,128)} %l_hbm.1, f32[2,96,384]{2,1,0:T(8,128)} %b_hbm.1, f32[48,6144]{1,0:T(8,128)} %k_hbm.1, f32[2,6,128,128]{3,2,1,0:T(8,128)} %c_hbm.1, s32[6,2,128]{2,1,0:T(2,128)} %bitcast.6, ...), custom_call_target="tpu_custom_call" | custom-call | tf_op jit(solution)/shard_map/schwarz/pallas_call | solution.py:675
  106.0 2.1 %multiply_bitcast_fusion = (f32[2,384,128]{2,1,0:T(8,128)}, f32[2,384,128]{2,1,0:T(8,128)}) fusion(f32[2,2,384,128]{3,2,1,0:T(8,128)} %schwarz.1), kind=kLoop, calls=%fused_computation | loop fusion | flops 196608 | bytes 1572864 | tf_op jit(solution)/shard_map/mul | solution.py:726

commit v4 on v3

--- a/solution.py
+++ b/solution.py
@@ -69,19 +69,31 @@
     def zat(k):
         return (lax.rem(z + k, 8), y, cr, cc)
 
-    counter = [0]
-    pending = []
-
-    def remote(src, dst, dev, keep=True):
-        i = counter[0]
-        counter[0] += 1
-        c = pltpu.make_async_remote_copy(
-            src_ref=src, dst_ref=dst, send_sem=ss.at[i], recv_sem=rs.at[i],
+    n_send = [0]
+    n_recv = [0]
+    tail = []
+
+    def slot(count):
+        i = count[0]
+        count[0] += 1
+        return i
+
+    def remote(src, dst, dev, si, ri):
+        return pltpu.make_async_remote_copy(
+            src_ref=src, dst_ref=dst, send_sem=ss.at[si], recv_sem=rs.at[ri],
             device_id=dev, device_id_type=pl.DeviceIdType.MESH,
         )
-        if keep:
-            pending.append(c)
-        return c
+
+    def take_recv(ref, ri):
+        remote(ref, ref, sib, 0, ri).wait_recv()
+
+    def take_send(ref, si):
+        remote(ref, ref, sib, si, 0).wait_send()
+
+    def send_slot(ref):
+        i = slot(n_send)
+        tail.append((ref, i))
+        return i
 
     def load(i, src, dst):
         c = pltpu.make_async_copy(src, dst, ldsem.at[i])
@@ -169,11 +181,16 @@
     def coarse_copies(it):
         q = {}
         g = rhs.at[it]
-        first = counter[0]
-
-        def block(zz, yy, half, dev):
+        first = n_recv[0]
+        links = [slot(n_send), slot(n_send)]
+        chip = send_slot(g.at[pl.ds(0, 4)])
+
+        def block(zz, yy, half, dev, si, ri):
             b = g.at[zz, yy, half]
-            return remote(b, b, dev, False)
+            return remote(b, b, dev, si, ri)
+
+        def link(zz, yy, half, dev, way):
+            return block(zz, yy, half, dev, links[way], slot(n_recv))
 
         def zm(k):
             return lax.rem(z + 8 + k, 8)
@@ -182,52 +199,57 @@
             return lax.rem(y + 4 + k, 4)
 
         for k in (1, 3, 2):
-            q["y", k] = block(z, y, 0, yat(k))
+            q["y", k] = link(z, y, 0, yat(k), 0)
         for j in range(4):
             for h in range(1, 5):
                 if h < 4 or j < 2:
-                    q["p", j, h] = block(zm(1 - h), ym(-j), 0, zat(1))
+                    q["p", j, h] = link(zm(1 - h), ym(-j), 0, zat(1), 1)
                 if h < 4 or j >= 2:
-                    q["m", j, h] = block(zm(h - 1), ym(-j), 0, zat(7))
+                    q["m", j, h] = link(zm(h - 1), ym(-j), 0, zat(7), 1)
         keys0 = list(q)
-        last = counter[0]
-        counter[0] = first
+        last = n_recv[0]
+        n_recv[0] = first
         for h in range(1, 5):
-            q["s", h] = block(zm(1 - h), y, 1, zat(1))
+            q["s", h] = link(zm(1 - h), y, 1, zat(1), 0)
             if h < 4:
-                q["t", h] = block(zm(h - 1), y, 1, zat(7))
+                q["t", h] = link(zm(h - 1), y, 1, zat(7), 0)
         for k in range(8):
             for h in range(1, 3):
                 if h < 2 or k % 2 == 0:
-                    q["u", k, h] = block(zm(-k), ym(1 - h), 1, yat(1))
+                    q["u", k, h] = link(zm(-k), ym(1 - h), 1, yat(1), 1)
                 if h < 2 or k % 2 == 1:
-                    q["v", k, h] = block(zm(-k), ym(h - 1), 1, yat(3))
+                    q["v", k, h] = link(zm(-k), ym(h - 1), 1, yat(3), 1)
         keys1 = [k for k in q if k not in keys0]
-        counter[0] = max(last, counter[0])
-        q["c0"] = [q[k] for k in keys0]
-        q["c1"] = [q[k] for k in keys1]
+        n_recv[0] = max(last, n_recv[0])
+        chips = [slot(n_recv), slot(n_recv)]
         f0 = {}
-        f0["y", 0] = block(z, y, 0, sib)
-        for k in (1, 2, 3):
-            f0["y", k] = block(z, ym(-k), 0, sib)
+        def chip0(key, zz, yy):
+            f0[key] = block(zz, yy, 0, sib, chip, chips[key[-1] == 4])
+
+        def chip1(key, zz, yy):
+            f1[key] = block(zz, yy, 1, sib, chip, chips[key[1] == 4])
+
+        for k in range(4):
+            chip0(("y", k), z, ym(-k))
         for key in keys0:
             if key[0] == "p":
-                f0[key] = block(zm(-key[2]), ym(-key[1]), 0, sib)
+                chip0(key, zm(-key[2]), ym(-key[1]))
             if key[0] == "m":
-                f0[key] = block(zm(key[2]), ym(-key[1]), 0, sib)
+                chip0(key, zm(key[2]), ym(-key[1]))
         f1 = {}
-        f1["z", 0] = block(z, y, 1, sib)
-        for k in range(1, 8):
-            f1["z", k] = block(zm(-k), y, 1, sib)
+        for k in range(8):
+            chip1(("z", k), zm(-k), y)
         for key in keys1:
             if key[0] == "u":
-                f1[key] = block(zm(-key[1]), ym(-key[2]), 1, sib)
+                chip1(key, zm(-key[1]), ym(-key[2]))
             if key[0] == "v":
-                f1[key] = block(zm(-key[1]), ym(key[2]), 1, sib)
+                chip1(key, zm(-key[1]), ym(key[2]))
+        assert len(f0) == len(f1) == 32
         q["f0"] = f0
         q["f1"] = f1
-        q["c0"] = q["c0"] + list(f0.values())
-        q["c1"] = q["c1"] + list(f1.values())
+        q["links"] = links
+        q["chips"] = chips
+        q["g"] = g
         return q
 
     def coarse_step(q, n):
@@ -268,10 +290,6 @@
                     relay(f, "p", "m", j, [n - 2])
                 if n < 5:
                     relay(f, "p", "m", 0, [n])
-            if n >= 7:
-                for key, c in q["f1"].items():
-                    if (key[1] == 4) == (n == 8):
-                        c.wait_recv()
 
         @pl.when(co == 1)
         def _():
@@ -303,36 +321,43 @@
                 both(n - 1, 1)
             if 2 <= n <= 6:
                 both(n - 2, 2)
-            if n >= 7:
-                for key, c in q["f0"].items():
-                    if (key[-1] == 4) == (n == 8):
-                        c.wait_recv()
+
+        if n == 7:
+            take_recv(q["g"].at[pl.ds(0, 7), :, 0], q["chips"][0])
+        if n == 8:
+            take_recv(q["g"].at[0, :, 0], q["chips"][1])
 
     def coarse_drain(q):
+        g = q["g"]
+
         @pl.when(co == 0)
         def _():
-            for c in q["c0"]:
-                c.wait_send()
+            take_send(g.at[0, pl.ds(0, 3), 0], q["links"][0])
+            take_send(g.at[pl.ds(0, 7), :, 0], q["links"][1])
 
         @pl.when(co == 1)
         def _():
-            for c in q["c1"]:
-                c.wait_send()
+            take_send(g.at[pl.ds(0, 7), 0, 0], q["links"][0])
+            take_send(g.at[pl.ds(0, 3)], q["links"][1])
 
     def gather_copies(buf, order=(0, 1)):
-        g = {"own": [], "opp": [], "fwd": []}
+        g = {"own": [], "opp": [], "fwd": [], "near": [], "far": [], "buf": buf}
+        si = send_slot(buf.at[:, pl.ds(0, 3)])
         for s in order:
-            g["own"].append(remote(buf.at[s, cr], buf.at[s, cr], sib))
+            near = slot(n_recv)
+            far = slot(n_recv)
+            g["near"].append(near)
+            g["far"].append(far)
+            g["own"].append(remote(buf.at[s, cr], buf.at[s, cr], sib, si, near))
             g["opp"].append([])
             for h in range(2):
                 b = buf.at[s, cr, pl.ds(192 * h, 192)]
-                g["opp"][-1].append(remote(b, b, opp))
-            g["fwd"].append(remote(buf.at[s, oc], buf.at[s, oc], sib))
+                g["opp"][-1].append(remote(b, b, opp, si, far))
+            g["fwd"].append(remote(buf.at[s, oc], buf.at[s, oc], sib, si, near))
         return g
 
     def forward(g, s):
-        for c in g["opp"][s]:
-            c.wait_recv()
+        take_recv(g["buf"].at[0, 0], g["far"][s])
         g["fwd"][s].start()
 
     def send(g, s):
@@ -341,16 +366,14 @@
         g["own"][s].start()
 
     def arrived(g, s):
-        g["own"][s].wait_recv()
-        g["fwd"][s].wait_recv()
+        take_recv(g["buf"].at[0, pl.ds(0, 2)], g["near"][s])
 
     def combine():
-        cs = []
+        si = send_slot(pin)
+        ri = slot(n_recv)
         for i, (half, dev) in enumerate(((1 - co, sib), (co, opp), (1 - co, ops))):
-            c = remote(part.at[half], pin.at[i], dev)
-            c.start()
-            cs.append(c)
-        return cs
+            remote(part.at[half], pin.at[i], dev, si, ri).start()
+        return ri
 
     def solve_group(it, off):
         i = lax.rem(z + off, 8)
@@ -365,10 +388,11 @@
 
     def solve_rest(it, acc):
         co48[it, cr] = quad(acc + solve_group(it, 4), 48)
-        cs = [remote(co48.at[it, cr], co48.at[it, cr], dev) for dev in (opp, ops, sib)]
-        for c in cs:
-            c.start()
-        return cs
+        si = send_slot(co48.at[it, pl.ds(0, 3)])
+        ri = slot(n_recv)
+        for dev in (opp, ops, sib):
+            remote(co48.at[it, cr], co48.at[it, cr], dev, si, ri).start()
+        return ri
 
     def weights(it, s):
         first = co48[it, pl.ds(2 * s, 2)].reshape(96, 128)
@@ -425,12 +449,21 @@
         pl.semaphore_wait(bar, 11)
 
     c_part = combine()
-    c_list_dn = remote(lists.at[pl.ds(0, 2)], rl.at[0], dn)
-    c_list_up = remote(lists.at[pl.ds(2, 2)], rl.at[1], up)
-    c_b1 = remote(bf.at[1 - cc, cr, pl.ds(0, 96)], bf.at[1 - cc, cr, pl.ds(0, 96)], otwin)
-    c_b2 = remote(bf.at[cc, oc, pl.ds(0, 96)], bf.at[cc, oc, pl.ds(0, 96)], twin)
-    c_bs = remote(bf.at[:, cr, pl.ds(0, 96)], bf.at[:, cr, pl.ds(0, 96)], sib)
-    c_bo = remote(bf.at[:, oc, pl.ds(0, 96)], bf.at[:, oc, pl.ds(0, 96)], sib)
+    s_list = send_slot(rl)
+    r_list = slot(n_recv)
+    c_list_dn = remote(lists.at[pl.ds(0, 2)], rl.at[0], dn, s_list, r_list)
+    c_list_up = remote(lists.at[pl.ds(2, 2)], rl.at[1], up, s_list, r_list)
+    s_b = send_slot(bf.at[:, pl.ds(0, 3), pl.ds(0, 96)])
+    r_b = [slot(n_recv) for _ in range(3)]
+
+    def basis(at, dev, ri):
+        b = bf.at[at + (pl.ds(0, 96),)]
+        return remote(b, b, dev, s_b, r_b[ri])
+
+    c_b1 = basis((1 - cc, cr), otwin, 0)
+    c_b2 = basis((cc, oc), twin, 1)
+    c_bs = basis((slice(None), cr), sib, 2)
+    c_bo = basis((slice(None), oc), sib, 2)
     c_b1.start()
     gr = gather_copies(rb.at[0])
     for s in range(2):
@@ -451,8 +484,7 @@
     conv_matrix(0, 1)
     ld_s1 = load(7, s_hbm.at[1], stage.at[1])
 
-    for c in c_part:
-        c.wait_recv()
+    take_recv(pin, c_part)
     rhs[0, z, y, co] = (part[co] + pin[0]) + (pin[1] + pin[2])
     q = coarse_copies(0)
     coarse_step(q, 0)
@@ -460,8 +492,7 @@
     hi, lo = split(kst[...])
     km[0:48] = hi
     km[48:96] = lo
-    c_list_dn.wait_recv()
-    c_list_up.wait_recv()
+    take_recv(rl, r_list)
     build_pick(0, lambda k: rl[0, 0, pl.ds(k, 1), :])
     coarse_step(q, 1)
     build_pick(1, lambda k: rl[1, 0, pl.ds(k, 1), :])
@@ -502,8 +533,7 @@
     c_b2.wait_recv()
     c_bo.start()
     build_scatter(1)
-    c_bs.wait_recv()
-    c_bo.wait_recv()
+    take_recv(bf.at[:, pl.ds(0, 2), pl.ds(0, 96)], r_b[2])
     lax.fori_loop(0, 4, lambda j, carry: (build_bt(j), carry)[1], 0)
     for j in range(4):
         hi, lo = split(bf[co, j, 0:96, :])
@@ -518,10 +548,13 @@
     for it in range(ITERS):
         c_up = []
         c_dn = []
+        s_ps = send_slot(ps.at[it])
+        r_fr = []
         for g in range(2):
             part_rows = pl.ds(384 * g, 384)
-            c_up.append(remote(ps.at[it, 0, part_rows], fr.at[it, 0, part_rows], up))
-            c_dn.append(remote(ps.at[it, 1, part_rows], fr.at[it, 1, part_rows], dn))
+            r_fr.append(slot(n_recv))
+            c_up.append(remote(ps.at[it, 0, part_rows], fr.at[it, 0, part_rows], up, s_ps, r_fr[g]))
+            c_dn.append(remote(ps.at[it, 1, part_rows], fr.at[it, 1, part_rows], dn, s_ps, r_fr[g]))
         if it == 1:
             arrived(gl, 0)
             arrived(gl, 1)
@@ -533,8 +566,7 @@
                 ps[1, 1, rows] = pick(1, 0, g)
                 ps[1, 0, rows] = pick(0, 1, g)
                 ps[1, co, rows] = ps[1, co, rows] + pick(2, co, g)
-            for c in cs:
-                c.wait_recv()
+            take_recv(co48.at[it, pl.ds(0, 3)], cs)
             ws = [weights(1, 1), weights(1, 0), weights(1, co)]
             for g in range(2):
                 rows = slice(384 * g, 384 * (g + 1))
@@ -545,8 +577,7 @@
             rebuild(1, 0)
             rebuild(1, 1)
         if it == 0:
-            for c in cs:
-                c.wait_recv()
+            take_recv(co48.at[it, pl.ds(0, 3)], cs)
             arrived(gl, 0)
             rebuild(0, 0)
             forward(gl, 1)
@@ -582,29 +613,27 @@
             for s in range(2):
                 res[s] = r1[s] - damping * apply(1, s)
         own_rows = [pick(3, 1 - co, g) for g in range(2)]
-        c_tm = []
+        s_tm = send_slot(tm.at[it, 0])
+        r_tm = slot(n_recv)
         for g in range(2):
             if it == 0:
                 for m, src_s in ((0, 1), (1, 0)) if g == 0 else ((2, co),):
                     for h in range(2):
                         rows = slice(384 * h, 384 * (h + 1))
                         qm[m, rows] = mm(pickm[m, rows], bt[src_s]).astype(bf16)
-            c_up[g].wait_recv()
-            c_dn[g].wait_recv()
             part_rows = pl.ds(384 * g, 384)
+            take_recv(fr.at[it, :, part_rows], r_fr[g])
             src = own_rows[g] + fr[it, 0, part_rows] + fr[it, 1, part_rows]
             for k in range(3):
                 rows = slice(384 * g + 128 * k, 384 * g + 128 * (k + 1))
                 tm[it, co, rows, :] = quad(
                     mm(cm[3 * g + k], wide(src[128 * k:128 * (k + 1)])), 128
                 )
-            c = remote(tm.at[it, co, part_rows], tm.at[it, co, part_rows], sib)
-            c.start()
-            c_tm.append(c)
+            terms = tm.at[it, co, part_rows]
+            remote(terms, terms, sib, s_tm, r_tm).start()
             if it == 0:
                 forward(gy, g)
-        for c in c_tm:
-            c.wait_recv()
+        take_recv(tm.at[it, 0], r_tm)
         tx = [wide(tm[it, s]) for s in range(2)]
         own = pl.ds(pl.multiple_of(cr * 384, 384), 384)
         for s in range(2):
@@ -650,11 +679,13 @@
             coarse_step(q, 8)
             cs = solve_rest(1, acc)
     coarse_drain(q)
-    for c in pending:
-        c.wait_send()
-
-
-N_COPIES = 260
+    for ref, i in tail:
+        take_send(ref, i)
+    assert n_send[0] == N_SEND and n_recv[0] == N_RECV, (n_send, n_recv)
+
+
+N_SEND = 19
+N_RECV = 95
 
 
 def per_device(
@@ -712,8 +743,8 @@
             pltpu.SMEM((2,), jnp.int32),
             V((5, 8, 128), jnp.int32),
             pltpu.SemaphoreType.DMA((12,)),
-            pltpu.SemaphoreType.DMA((N_COPIES,)),
-            pltpu.SemaphoreType.DMA((N_COPIES,)),
+            pltpu.SemaphoreType.DMA((N_SEND,)),
+            pltpu.SemaphoreType.DMA((N_RECV,)),
         ],
         compiler_params=pltpu.CompilerParams(
             collective_id=0, has_side_effects=True, vmem_limit_bytes=66_000_000

time: 108 us -> 104 us (0.963)
  Pallas kernels: 105 us -> 101 us
    pallas_call x1, Pallas kernels: 105 us -> 101 us  [per_device(): pl.pallas_call(kernel, name='schwarz', out_shape=jax.ShapeDtypeStruct((2,...]
where the time goes in v4:
time: 104 us
  Pallas kernels  101 us (97%)
  other arithmetic  2.05 us (2%)
    pallas_call x1, Pallas kernels, per_device(): pl.pallas_call(kernel, name='schwarz', out_shape=jax.ShapeDtypeStruct((2,...  101 us

profile of v4, /device:TPU:1, one launch (start us, length us, event | category | flops | bytes accessed | tf_op | source)
XLA Modules:
  0.0 103.5 jit_solution(9359743546621806982)
XLA Ops:
  0.6 100.8 %schwarz.1 = f32[2,2,384,128]{3,2,1,0:T(8,128)} custom-call(f32[2,384,128]{2,1,0:T(8,128)} %r_hbm.1, f32[2,384,1536]{2,1,0:T(8,128)} %s_hbm.1, f32[2,384,1536]{2,1,0:T(8,128)} %l_hbm.1, f32[2,96,384]{2,1,0:T(8,128)} %b_hbm.1, f32[48,6144]{1,0:T(8,128)} %k_hbm.1, f32[2,6,128,128]{3,2,1,0:T(8,128)} %c_hbm.1, s32[6,2,128]{2,1,0:T(2,128)} %bitcast.6, ...), custom_call_target="tpu_custom_call" | custom-call | tf_op jit(solution)/shard_map/schwarz/pallas_call | solution.py:706
  101.5 2.1 %multiply_bitcast_fusion = (f32[2,384,128]{2,1,0:T(8,128)}, f32[2,384,128]{2,1,0:T(8,128)}) fusion(f32[2,2,384,128]{3,2,1,0:T(8,128)} %schwarz.1), kind=kLoop, calls=%fused_computation | loop fusion | flops 196608 | bytes 1572864 | tf_op jit(solution)/shard_map/mul | solution.py:757

commit v5 on v4

--- a/solution.py
+++ b/solution.py
@@ -566,10 +566,9 @@
                 ps[1, 1, rows] = pick(1, 0, g)
                 ps[1, 0, rows] = pick(0, 1, g)
                 ps[1, co, rows] = ps[1, co, rows] + pick(2, co, g)
-            take_recv(co48.at[it, pl.ds(0, 3)], cs)
-            ws = [weights(1, 1), weights(1, 0), weights(1, co)]
-            for g in range(2):
-                rows = slice(384 * g, 384 * (g + 1))
+                if g == 0:
+                    take_recv(co48.at[it, pl.ds(0, 3)], cs)
+                    ws = [weights(1, 1), weights(1, 0), weights(1, co)]
                 for m, dest in ((0, 0), (1, 1), (2, co)):
                     ps[1, dest, rows] = ps[1, dest, rows] + halves(mm(qm[m, rows], ws[m]))
                 c_up[g].start()
@@ -614,7 +613,8 @@
                 res[s] = r1[s] - damping * apply(1, s)
         own_rows = [pick(3, 1 - co, g) for g in range(2)]
         s_tm = send_slot(tm.at[it, 0])
-        r_tm = slot(n_recv)
+        r_tm = [slot(n_recv), slot(n_recv)]
+        own = pl.ds(pl.multiple_of(cr * 384, 384), 384)
         for g in range(2):
             if it == 0:
                 for m, src_s in ((0, 1), (1, 0)) if g == 0 else ((2, co),):
@@ -622,6 +622,11 @@
                         rows = slice(384 * h, 384 * (h + 1))
                         qm[m, rows] = mm(pickm[m, rows], bt[src_s]).astype(bf16)
             part_rows = pl.ds(384 * g, 384)
+            if g == 1:
+                take_recv(tm.at[it, 0, pl.ds(0, 384)], r_tm[0])
+                early = [
+                    halves(mm(tt[s, own, 0:384], wide(tm[it, s, 0:384]))) for s in range(2)
+                ]
             take_recv(fr.at[it, :, part_rows], r_fr[g])
             src = own_rows[g] + fr[it, 0, part_rows] + fr[it, 1, part_rows]
             for k in range(3):
@@ -630,14 +635,13 @@
                     mm(cm[3 * g + k], wide(src[128 * k:128 * (k + 1)])), 128
                 )
             terms = tm.at[it, co, part_rows]
-            remote(terms, terms, sib, s_tm, r_tm).start()
+            remote(terms, terms, sib, s_tm, r_tm[g]).start()
             if it == 0:
                 forward(gy, g)
-        take_recv(tm.at[it, 0], r_tm)
-        tx = [wide(tm[it, s]) for s in range(2)]
-        own = pl.ds(pl.multiple_of(cr * 384, 384), 384)
+        take_recv(tm.at[it, 0, pl.ds(0, 384)], r_tm[1])
         for s in range(2):
-            own_inflow = halves(mm(tt[s, own, :], tx[s]))
+            late = halves(mm(tt[s, own, 384:768], wide(tm[it, s, 384:768])))
+            own_inflow = early[s] + late
             if it == 0:
                 r1[s] = rb[1, s, cr] + damping * own_inflow
                 store_x(s, cr, r1[s])
@@ -685,7 +689,7 @@
 
 
 N_SEND = 19
-N_RECV = 95
+N_RECV = 97
 
 
 def per_device(

time: 104 us -> 104 us (level)
  no operation moved by 1% of the time
where the time goes in v5:
time: 104 us; the launch traced here: 103 us
  Pallas kernels  101 us (97%)
  other arithmetic  2.05 us (2%)
    pallas_call x1, Pallas kernels, per_device(): pl.pallas_call(kernel, name='schwarz', out_shape=jax.ShapeDtypeStruct((2,...  101 us

profile of v5, /device:TPU:1, one launch (start us, length us, event | category | flops | bytes accessed | tf_op | source)
XLA Modules:
  0.0 103.5 jit_solution(17458418271175651792)
XLA Ops:
  0.6 100.8 %schwarz.1 = f32[2,2,384,128]{3,2,1,0:T(8,128)} custom-call(f32[2,384,128]{2,1,0:T(8,128)} %r_hbm.1, f32[2,384,1536]{2,1,0:T(8,128)} %s_hbm.1, f32[2,384,1536]{2,1,0:T(8,128)} %l_hbm.1, f32[2,96,384]{2,1,0:T(8,128)} %b_hbm.1, f32[48,6144]{1,0:T(8,128)} %k_hbm.1, f32[2,6,128,128]{3,2,1,0:T(8,128)} %c_hbm.1, s32[6,2,128]{2,1,0:T(2,128)} %bitcast.6, ...), custom_call_target="tpu_custom_call" | custom-call | tf_op jit(solution)/shard_map/schwarz/pallas_call | solution.py:710
  101.4 2.1 %multiply_bitcast_fusion = (f32[2,384,128]{2,1,0:T(8,128)}, f32[2,384,128]{2,1,0:T(8,128)}) fusion(f32[2,2,384,128]{3,2,1,0:T(8,128)} %schwarz.1), kind=kLoop, calls=%fused_computation | loop fusion | flops 196608 | bytes 1572864 | tf_op jit(solution)/shard_map/mul | solution.py:761
